TPU v7x, 32 devices: a whole 2x2x4 slice. The times are simulated.
32 devices in a mesh: shot: 4 (over y, core), gx: 4 (over z), gy: 2 (over x).
Axes of the slice: x: 2, y: 2, z: 4, core: 2. Of those that a mesh axis runs over, the one named last changes fastest.
Arguments:
- latent: float32 [32, 24, 1024], P('shot', 'gx', 'gy'), may hold values from -6 to 6
- w_first: float32 [64, 64], replicated, may hold values from -0.75 to 0.75
- w_second: float32 [64, 128], replicated, may hold values from -0.75 to 0.75
- fwd_press: float32 [4, 96, 64, 128], P('shot', 'gx', 'gy'), may hold values from -1.5 to 8
- fwd_vel: float32 [4, 3, 96, 64, 128], P('shot', None, 'gx', 'gy'), may hold values from -1.5 to 8
- adj_press: float32 [4, 96, 64, 128], P('shot', 'gx', 'gy'), may hold values from -1.5 to 8
- adj_vel: float32 [4, 3, 96, 64, 128], P('shot', None, 'gx', 'gy'), may hold values from -1.5 to 8
- src_pos: int32 [3, 4], P(None, 'shot'), may hold values from 0 to 127, as said below
- src_amp: float32 [3, 4], P(None, 'shot'), may hold values from -24 to 24
- rec_pos: int32 [4, 3, 2048], P('shot'), may hold values from 0 to 127, as said below
- observed: float32 [4, 3, 2048], P('shot'), may hold values from -6 to 6
Outputs:
- grad_latent: float32 [32, 24, 1024], P('shot', 'gx', 'gy')
- grad_first: float32 [64, 64], replicated
- grad_second: float32 [64, 128], replicated
Inputs may be any that keep to these rules, and one draw needn't show every extreme that they name: `src_pos`: row 0 is an x cell below 96, row 1 a y cell below 64, row 2 a depth cell below 128. `rec_pos`: component 0 is an x cell below 96, component 1 a y cell below 64, component 2 a depth cell below 128; cells may repeat.
All inputs are finite; a program needn't handle non-finite values.
Results may differ from a plain program's by a relative error of at most 0.0003.
Values sent between devices are 32-bit elements; how exact they have to be, the bound alone decides.
A program may use at most 64 MiB of HBM per device.

v0:
```python
import jax
import jax.numpy as jnp
from jax import lax
from jax.sharding import PartitionSpec as P

CH = 64
STEPS = 3
coeffs = (1225.0 / 1024.0, -245.0 / 3072.0, 49.0 / 5120.0, -5.0 / 7168.0)


def with_halo(block, sides, width):
    for axis, dim in sides:
        count = lax.axis_size(axis)
        forward = [(i, i + 1) for i in range(count - 1)]
        backward = [(target, source) for source, target in forward]
        low = lax.ppermute(
            lax.slice_in_dim(block, block.shape[dim] - width, None, axis=dim), axis, forward
        )
        high = lax.ppermute(lax.slice_in_dim(block, 0, width, axis=dim), axis, backward)
        block = jnp.concatenate([low, block, high], axis=dim)
    return block


def take_slab(values_in, axis_id, start_at, length):
    return lax.slice_in_dim(values_in, start_at, start_at + length, axis=axis_id)


def diff_plus(extended, axis_id, start_at, length):
    summed = 0.0
    for order, weight in enumerate(coeffs):
        offset = order + 1
        summed = summed + weight * (
            take_slab(extended, axis_id, start_at + offset, length)
            - take_slab(extended, axis_id, start_at - offset + 1, length)
        )
    return summed


def diff_minus(extended, axis_id, start_at, length):
    summed = 0.0
    for order, weight in enumerate(coeffs):
        offset = order + 1
        summed = summed + weight * (
            take_slab(extended, axis_id, start_at + offset - 1, length)
            - take_slab(extended, axis_id, start_at - offset, length)
        )
    return summed


def depth_pad(field_in):
    return jnp.pad(field_in, ((0, 0), (0, 0), (4, 4)))


def rim_x(field_in):
    return with_halo(field_in, (("gx", 0),), 4)


def rim_y(field_in):
    return with_halo(field_in, (("gy", 1),), 4)


def wide_step(fields, modulus, buoy_x, buoy_y, buoyancy):
    pressure, ext_x, ext_y, vel_z = fields
    size_x, size_y, size_z = pressure.shape
    slope_x = diff_plus(with_halo(pressure, (("gx", 0),), 8), 0, 4, size_x + 8)
    slope_y = diff_plus(with_halo(pressure, (("gy", 1),), 8), 1, 4, size_y + 8)
    grad_z = diff_plus(depth_pad(pressure), 2, 4, size_z)
    ext_x = ext_x - buoy_x * slope_x
    ext_y = ext_y - buoy_y * slope_y
    vel_z = vel_z - buoyancy * grad_z
    diverge = (
        diff_minus(ext_x, 0, 4, size_x)
        + diff_minus(ext_y, 1, 4, size_y)
        + diff_minus(depth_pad(vel_z), 2, 4, size_z)
    )
    pressure = pressure - modulus * diverge
    slopes = (slope_x[4 : 4 + size_x], slope_y[:, 4 : 4 + size_y], grad_z)
    own_vel = (ext_x[4 : 4 + size_x], ext_y[:, 4 : 4 + size_y], vel_z)
    return ((pressure, ext_x, ext_y, vel_z), diverge, slopes, own_vel)


def decode(latent, w_first, w_second):
    depth_c, rows_x, merged = latent.shape
    rows_y = merged // CH
    flattened = latent.reshape(-1, CH)
    hidden = jnp.tanh(jnp.dot(flattened, w_first, precision=lax.Precision.HIGHEST))
    outputs = jnp.dot(hidden, w_second, precision=lax.Precision.HIGHEST)
    fine_out = (
        outputs.reshape(depth_c, rows_x, rows_y, 2, 4, 4, 4)
        .transpose(3, 1, 4, 2, 5, 0, 6)
        .reshape(2, rows_x * 4, rows_y * 4, depth_c * 4)
    )
    return (flattened, hidden, fine_out)


def materials(fine_out):
    wave_speed = 0.15 + 0.25 * jax.nn.sigmoid(fine_out[0])
    density = 1.0 + 1.5 * jax.nn.sigmoid(fine_out[1])
    return (density * wave_speed * wave_speed, 1.0 / density)


def decoder_grads(flattened, hidden, fine_out, grad_mod, grad_buoy, w_first, w_second):
    sig_speed = jax.nn.sigmoid(fine_out[0])
    sig_dens = jax.nn.sigmoid(fine_out[1])
    wave_speed = 0.15 + 0.25 * sig_speed
    density = 1.0 + 1.5 * sig_dens
    grad_speed = grad_mod * 2.0 * density * wave_speed
    grad_dens = grad_mod * wave_speed * wave_speed - grad_buoy / (density * density)
    grad_fine = jnp.stack(
        [
            grad_speed * 0.25 * sig_speed * (1.0 - sig_speed),
            grad_dens * 1.5 * sig_dens * (1.0 - sig_dens),
        ]
    )
    size_x, size_y, size_z = (grad_fine.shape[1], grad_fine.shape[2], grad_fine.shape[3])
    grad_out = (
        grad_fine.reshape(2, size_x // 4, 4, size_y // 4, 4, size_z // 4, 4)
        .transpose(5, 1, 3, 0, 2, 4, 6)
        .reshape(-1, 128)
    )
    grad_hidden = jnp.dot(grad_out, w_second.T, precision=lax.Precision.HIGHEST)
    grad_pre = grad_hidden * (1.0 - hidden * hidden)
    grad_latent = jnp.dot(grad_pre, w_first.T, precision=lax.Precision.HIGHEST).reshape(
        size_z // 4, size_x // 4, size_y // 4 * CH
    )
    grad_second = jnp.dot(hidden.T, grad_out, precision=lax.Precision.HIGHEST)
    grad_first = jnp.dot(flattened.T, grad_pre, precision=lax.Precision.HIGHEST)
    return (grad_latent, grad_first, grad_second)


def receiver_fields(receivers, observed_now, anchor_x, anchor_y, size_x, size_y, size_z):
    local_x = receivers[0] - anchor_x
    local_y = receivers[1] - anchor_y
    inside = (local_x >= 0) & (local_x < size_x) & (local_y >= 0) & (local_y < size_y)
    column = jnp.where(inside, local_x * size_y + local_y, -1)
    count = column.shape[0]
    picks = (
        lax.broadcasted_iota(jnp.int32, (size_x * size_y, count), 0) == column[None, :]
    ).astype(jnp.bfloat16)
    depth = (lax.broadcasted_iota(jnp.int32, (count, size_z), 1) == receivers[2][:, None]).astype(
        jnp.float32
    )
    high = lax.reduce_precision(observed_now, 8, 7)
    low = lax.reduce_precision(observed_now - high, 8, 7)
    parts = [depth]
    for moment in range(STEPS):
        parts = parts + [depth * high[moment][:, None], depth * low[moment][:, None]]
    weights = jnp.concatenate(parts, axis=1).astype(jnp.bfloat16)
    summed = jnp.dot(picks, weights, preferred_element_type=jnp.float32)
    planes = summed.reshape(size_x, size_y, len(parts), size_z)
    recorded = [planes[:, :, 1 + 2 * m] + planes[:, :, 2 + 2 * m] for m in range(STEPS)]
    return (planes[:, :, 0], recorded)


def body(
    latent,
    w_first,
    w_second,
    fwd_press,
    fwd_vel,
    adj_press,
    adj_vel,
    src_pos,
    src_amp,
    rec_pos,
    observed,
):
    size_x, size_y = (fwd_press.shape[1], fwd_press.shape[2])
    anchor_x = lax.axis_index("gx") * size_x
    anchor_y = lax.axis_index("gy") * size_y
    flattened, hidden, fine_out = decode(latent, w_first, w_second)
    slab_mod, slab_buoy = materials(fine_out)
    stacked = lax.all_gather(jnp.stack([slab_mod, slab_buoy]), "shot", axis=3, tiled=True)
    modulus, buoyancy = (stacked[0], stacked[1])
    buoy_x = rim_x(buoyancy)
    buoy_y = rim_y(buoyancy)

    def prepare(vel_x, vel_y):
        return (rim_x(vel_x), rim_y(vel_y))

    def advance(fields):
        return wide_step(fields, modulus, buoy_x, buoy_y, buoyancy)

    def one_shot(totals, inputs):
        grad_mod, grad_buoy = totals
        (
            start_press,
            start_vel,
            back_press,
            back_vel,
            source,
            amplitudes,
            receivers,
            observed_now,
        ) = inputs
        size_z = start_press.shape[2]
        at_source = (
            (lax.broadcasted_iota(jnp.int32, start_press.shape, 0) == source[0] - anchor_x)
            & (lax.broadcasted_iota(jnp.int32, start_press.shape, 1) == source[1] - anchor_y)
            & (lax.broadcasted_iota(jnp.int32, start_press.shape, 2) == source[2])
        )
        hits, recorded = receiver_fields(
            receivers, observed_now, anchor_x, anchor_y, size_x, size_y, size_z
        )
        fields = (start_press,) + prepare(start_vel[0], start_vel[1]) + (start_vel[2],)
        stored = []
        misfits = []
        for moment in range(STEPS):
            fields, diverge, slopes, own_vel = advance(fields)
            pressure = fields[0] + jnp.where(at_source, amplitudes[moment], 0.0)
            fields = (pressure,) + fields[1:]
            misfits.append(hits * pressure - recorded[moment])
            stored.append((diverge, slopes))
        fields = (back_press,) + prepare(back_vel[0], back_vel[1]) + (back_vel[2],)
        for moment in reversed(range(STEPS)):
            pressure = fields[0] + misfits[moment]
            fields, diverge, slopes, own_vel = advance((pressure,) + fields[1:])
            grad_mod = grad_mod - fields[0] * stored[moment][0]
            grad_buoy = grad_buoy - (
                own_vel[0] * stored[moment][1][0]
                + own_vel[1] * stored[moment][1][1]
                + own_vel[2] * stored[moment][1][2]
            )
        return ((grad_mod, grad_buoy), None)

    zeros = jnp.zeros(modulus.shape, jnp.float32)
    totals, _ignored = lax.scan(
        one_shot,
        (zeros, zeros),
        (fwd_press, fwd_vel, adj_press, adj_vel, src_pos.T, src_amp.T, rec_pos, observed),
    )
    shares = lax.psum_scatter(
        jnp.stack([totals[0], totals[1]]), "shot", scatter_dimension=3, tiled=True
    )
    grad_latent, grad_first, grad_second = decoder_grads(
        flattened, hidden, fine_out, shares[0], shares[1], w_first, w_second
    )
    grad_first, grad_second = lax.psum((grad_first, grad_second), ("shot", "gx", "gy"))
    return (grad_latent, grad_first, grad_second)


def solution(mesh):
    in_specs = (
        P("shot", "gx", "gy"),
        P(),
        P(),
        P("shot", "gx", "gy", None),
        P("shot", None, "gx", "gy", None),
        P("shot", "gx", "gy", None),
        P("shot", None, "gx", "gy", None),
        P(None, "shot"),
        P(None, "shot"),
        P("shot", None, None),
        P("shot", None, None),
    )
    out_specs = (P("shot", "gx", "gy"), P(), P())
    return jax.shard_map(body, mesh=mesh, in_specs=in_specs, out_specs=out_specs, check_vma=False)
```

profile of v0, /device:TPU:0, one launch (start us, length us, event | category | flops | bytes accessed | tf_op | source)
XLA Modules:
  0.0 370.2 jit_solution(17085943684543270808)
XLA Ops:
  7.3 1.6 slice_bitcast_fusion.9
  8.9 5.6 %collective-permute-start = (f32[4,32,128]{2,1,0:T(8,128)}, f32[4,32,128]{2,1,0:T(8,128)}, u32[]{:S(2)}, u32[]{:S(2)}) collective-permute-start(f32[4,32,128]{2,1,0:T(8,128)} %get-tuple-element.116), channel_id=1, source_target_pairs={{0,2},{2,4},{4,6},{1,3},{3,5},{5,7},{8,10},{10,12},{12,14},{9,11},... | collective-permute-start | bytes 196616 | tf_op jit(solution)/shard_map/while/body/eval_jaxpr/ppermute | solution.py:16
  14.5 1.6 fusion.408
  16.1 4.0 %collective-permute-start.10 = (f32[24,8,128]{2,1,0:T(8,128)}, f32[24,8,128]{2,1,0:T(8,128)}, u32[]{:S(2)}, u32[]{:S(2)}) collective-permute-start(f32[24,8,128]{2,1,0:T(8,128)} %get-tuple-element.146), channel_id=1, source_target_pairs={{0,1},{2,3},{4,5},{6,7},{8,9},{10,11},{12,13},{14,15},{16,17},{18,... | collective-permute-start | bytes 294920 | tf_op jit(solution)/shard_map/while/body/eval_jaxpr/ppermute | solution.py:16
  21.4 1.9 slice_bitcast_fusion.3
  24.0 5.2 %collective-permute-start.6 = (f32[24,4,128]{2,1,0:T(4,128)}, f32[24,4,128]{2,1,0:T(4,128)S(1)}, u32[]{:S(2)}, u32[]{:S(2)}) collective-permute-start(f32[24,4,128]{2,1,0:T(4,128)} %get-tuple-element.152), channel_id=1, source_target_pairs={{0,1},{2,3},{4,5},{6,7},{8,9},{10,11},{12,13},{14,15},{16,17},{18,... | collective-permute-start | bytes 147464 | tf_op jit(solution)/shard_map/while/body/eval_jaxpr/ppermute | solution.py:16
  30.5 1.7 slice_bitcast_fusion.5
  32.2 1.5 slice_bitcast_fusion.7
  35.6 3.1 reshape.228
  38.7 4.9 %copy.58 = f32[8,6,8,2,4,4,4]{0,2,6,5,4,1,3:T(8,128)} copy(f32[8,6,8,2,4,4,4]{2,1,0,6,5,4,3:T(8,128)} %reshape.228) | data formatting | bytes 393216 | tf_op jit(solution)/shard_map/reshape | solution.py:89
  43.6 3.9 %fusion.4 = (f32[1,6,4,8,4,8,4]{5,3,6,4,2,1,0:T(8,128)}, f32[1,6,4,8,4,8,4]{5,3,6,4,2,1,0:T(8,128)S(1)}) fusion(f32[2,6,4,8,4,8,4]{5,3,6,4,2,1,0:T(8,128)} %bitcast.157), kind=kLoop, calls=%fused_computation.91 | loop fusion | flops 147456 | bytes 393216 | tf_op jit(solution)/shard_map/div | solution.py:97
  47.5 6.9 %copy.60 = f32[1,6,4,8,4,8,4]{6,5,4,3,2,1,0:T(8,128)} copy(f32[1,6,4,8,4,8,4]{5,3,6,4,2,1,0:T(8,128)} %get-tuple-element.108) | data formatting | bytes 196608 | tf_op jit(solution)/shard_map/div | solution.py:97
  54.4 2.4 div.74
  56.8 5.9 %copy.59 = f32[1,6,4,8,4,8,4]{6,5,4,3,2,1,0:T(8,128)} copy(f32[1,6,4,8,4,8,4]{5,3,6,4,2,1,0:T(8,128)S(1)} %get-tuple-element.109) | data formatting | bytes 196608 | tf_op jit(solution)/shard_map/div | solution.py:97
  62.6 2.4 div.72
  65.6 21.9 %all_gather.3 = f32[2,24,32,128]{2,1,0,3:T(8,128)S(1)} all-gather(f32[2,24,32,32]{2,1,0,3:T(8,128)S(1)} %copy.61), channel_id=1, replica_groups=mesh['shot'=4,'gx'=4,'gy'=2] {'shot'}, dimensions={3}, use_global_device_ids=true | all-gather | bytes 983040 | tf_op jit(solution)/shard_map/all_gather | solution.py:173
  87.7 1.9 fusion.394
  92.3 1.6 fusion.402
  99.8 5.0 %fusion = f32[768,896]{1,0:T(8,128)} fusion(bf16[2048,896]{1,0:T(8,128)(2,1)S(1)} %fusion.14, s32[2048]{0:T(1024)S(1)} %bitcast.183), kind=kOutput, calls=%fused_computation.2 | convolution fusion | flops 2820145152 | bytes 6430720 | tf_op jit(solution)/shard_map/while/body/eval_jaxpr/dot_general | solution.py:149
  104.8 4.1 %reshape.226 = f32[24,32,7,128]{3,2,1,0:T(8,128)} reshape(f32[768,896]{1,0:T(8,128)} %fusion) | data formatting | bytes 5505024 | tf_op jit(solution)/shard_map/while/body/eval_jaxpr/reshape | solution.py:150
  108.9 12.5 %slice_add_fusion = (f32[24,32,1,128]{3,2,1,0:T(1,128)}, f32[24,32,1,128]{3,2,1,0:T(1,128)}, f32[24,32,1,128]{3,2,1,0:T(1,128)}, f32[24,32,1,128]{3,2,1,0:T(1,12...) fusion(f32[24,32,7,128]{3,2,1,0:T(8,128)} %reshape.226), kind=kLoop, calls=%fused_computation.478 | loop fusion | flops 98304 | bytes 5111808 | tf_op jit(solution)/shard_map/while/body/eval_jaxpr/add | solution.py:151
  122.2 1.8 copy.80
  124.8 1.8 copy.82
  126.6 1.8 bitcast_subtract_fusion.2
  129.1 5.2 %collective-permute-start.8 = (f32[24,4,128]{2,1,0:T(4,128)S(1)}, f32[24,4,128]{2,1,0:T(4,128)S(1)}, u32[]{:S(2)}, u32[]{:S(2)}) collective-permute-start(f32[24,4,128]{2,1,0:T(4,128)S(1)} %get-tuple-element.148), channel_id=1, source_target_pairs={{0,1},{2,3},{4,5},{6,7},{8,9},{10,11},{12,13},{14,15},{16,17},{18,... | collective-permute-start | bytes 147464 | tf_op jit(solution)/shard_map/ppermute | solution.py:16
  136.5 1.4 collective-permute-start.1
  138.0 4.5 %collective-permute-start.20 = (f32[4,32,128]{2,1,0:T(8,128)}, f32[4,32,128]{2,1,0:T(8,128)S(1)}, u32[]{:S(2)}, u32[]{:S(2)}) collective-permute-start(f32[4,32,128]{2,1,0:T(8,128)} %get-tuple-element.112), channel_id=1, source_target_pairs={{0,2},{2,4},{4,6},{1,3},{3,5},{5,7},{8,10},{10,12},{12,14},{9,11},... | collective-permute-start | bytes 196616 | tf_op jit(solution)/shard_map/while/body/eval_jaxpr/ppermute | solution.py:16
  142.6 2.8 collective-permute-start.4
  145.5 1.4 collective-permute-start.5
  146.9 1.5 maximum_subtract_fusion.1
  149.7 3.0 collective-permute-done.5
  152.7 3.5 collective-permute-start.2
  157.5 4.7 %collective-permute-start.24 = (f32[24,4,128]{2,1,0:T(4,128)S(1)}, f32[24,4,128]{2,1,0:T(4,128)S(1)}, u32[]{:S(2)}, u32[]{:S(2)}) collective-permute-start(f32[24,4,128]{2,1,0:T(4,128)S(1)} %copy-done.19), channel_id=1, source_target_pairs={{0,1},{2,3},{4,5},{6,7},{8,9},{10,11},{12,13},{14,15},{16,17},{18,... | collective-permute-start | bytes 147464 | tf_op jit(solution)/shard_map/while/body/eval_jaxpr/ppermute | solution.py:16
  163.4 1.5 fusion.371
  169.2 4.5 %collective-permute-start.12 = (f32[8,32,128]{2,1,0:T(8,128)S(1)}, f32[8,32,128]{2,1,0:T(8,128)S(1)}, u32[]{:S(2)}, u32[]{:S(2)}) collective-permute-start(f32[8,32,128]{2,1,0:T(8,128)S(1)} %get-tuple-element.140), channel_id=1, source_target_pairs={{0,2},{2,4},{4,6},{1,3},{3,5},{5,7},{8,10},{10,12},{12,14},{9,11},... | collective-permute-start | bytes 393224 | tf_op jit(solution)/shard_map/while/body/eval_jaxpr/ppermute | solution.py:16
  176.3 4.8 %collective-permute-done.13 = f32[8,32,128]{2,1,0:T(8,128)S(1)} collective-permute-done((f32[8,32,128]{2,1,0:T(8,128)S(1)}, f32[8,32,128]{2,1,0:T(8,128)S(1)}, u32[]{:S(2)}, u32[]{:S(2)}) %collective-permute-start.13) | collective-permute-done | bytes 131104 | tf_op jit(solution)/shard_map/while/body/eval_jaxpr/ppermute | solution.py:19
  183.6 3.9 %collective-permute-start.18 = (f32[24,8,128]{2,1,0:T(8,128)S(1)}, f32[24,8,128]{2,1,0:T(8,128)S(1)}, u32[]{:S(2)}, u32[]{:S(2)}) collective-permute-start(f32[24,8,128]{2,1,0:T(8,128)S(1)} %get-tuple-element.138), channel_id=1, source_target_pairs={{0,1},{2,3},{4,5},{6,7},{8,9},{10,11},{12,13},{14,15},{16,17},{18,... | collective-permute-start | bytes 294920 | tf_op jit(solution)/shard_map/while/body/eval_jaxpr/ppermute | solution.py:16
  189.7 2.7 collective-permute-start.16
  192.4 1.6 collective-permute-done.19
  195.9 5.0 %collective-permute-done.17 = f32[8,32,128]{2,1,0:T(8,128)S(1)} collective-permute-done((f32[8,32,128]{2,1,0:T(8,128)S(1)}, f32[8,32,128]{2,1,0:T(8,128)S(1)}, u32[]{:S(2)}, u32[]{:S(2)}) %collective-permute-start.17) | collective-permute-done | bytes 131104 | tf_op jit(solution)/shard_map/while/body/eval_jaxpr/ppermute | solution.py:19
  202.2 1.6 fusion.369
  203.8 1.8 fusion.190
  205.6 2.7 collective-permute-start.26
  211.8 3.0 collective-permute-done.27
  214.8 3.5 collective-permute-start.22
  220.8 4.6 %collective-permute-done.23 = f32[8,32,128]{2,1,0:T(8,128)S(1)} collective-permute-done((f32[8,32,128]{2,1,0:T(8,128)S(1)}, f32[8,32,128]{2,1,0:T(8,128)S(1)}, u32[]{:S(2)}, u32[]{:S(2)}) %collective-permute-start.23) | collective-permute-done | bytes 131104 | tf_op jit(solution)/shard_map/while/body/eval_jaxpr/ppermute | solution.py:19
  228.1 1.5 collective-permute-start.30
  231.0 1.9 collective-permute-start.28
  234.2 1.9 collective-permute-done.31
  236.7 3.1 collective-permute-done.29
  241.7 4.6 %collective-permute-start.34 = (f32[24,8,128]{2,1,0:T(8,128)S(1)}, f32[24,8,128]{2,1,0:T(8,128)S(1)}, u32[]{:S(2)}, u32[]{:S(2)}) collective-permute-start(f32[24,8,128]{2,1,0:T(8,128)S(1)} %get-tuple-element.124), channel_id=1, source_target_pairs={{0,1},{2,3},{4,5},{6,7},{8,9},{10,11},{12,13},{14,15},{16,17},{18,... | collective-permute-start | bytes 294920 | tf_op jit(solution)/shard_map/while/body/eval_jaxpr/ppermute | solution.py:16
  247.6 1.9 collective-permute-start.32
  249.5 1.5 collective-permute-start.33
  251.0 1.7 collective-permute-done.35
  253.3 3.1 collective-permute-done.33
  258.5 2.2 copy.76
  260.7 3.4 reshape.234
  264.2 21.8 %reduce-scatter.4.cloned.1.call-done = f32[32,1536]{1,0:T(8,128)} async-done(((f32[128,1536]{1,0:T(8,128)}), f32[32,1536]{1,0:T(8,128)}) %reduce-scatter.4.cloned.1.call-update) | async-done | bytes 196624
  287.8 2.7 stack.27
  290.5 2.7 stack.28
  293.2 6.8 %maximum_bitcast_fusion = f32[8,6,8,2,4,4,4]{6,0,5,2,4,1,3:T(8,128)} fusion(f32[1,6,4,8,4,8,4]{6,5,4,3,2,1,0:T(8,128)} %stack.28, f32[1,6,4,8,4,8,4]{6,5,4,3,2,1,0:T(8,128)} %stack.27), kind=kLoop, calls=%fused_computation | loop fusion | flops 49152 | bytes 393216 | tf_op jit(solution)/shard_map/transpose | solution.py:118
  300.0 17.0 %copy.70 = f32[8,6,8,2,4,4,4]{2,1,0,6,5,4,3:T(8,128)} copy(f32[8,6,8,2,4,4,4]{6,0,5,2,4,1,3:T(8,128)} %maximum_bitcast_fusion) | data formatting | bytes 393216 | tf_op jit(solution)/shard_map/transpose | solution.py:118
  316.9 2.9 reshape.229
  321.3 40.3 %all-reduce.12 = (f32[64,64]{0,1:T(8,128)S(1)}, f32[64,128]{1,0:T(8,128)}) all-reduce(f32[64,64]{0,1:T(8,128)S(1)} %convolution_bitcast_fusion, f32[64,128]{1,0:T(8,128)S(1)} %fusion.417), channel_id=1, replica_groups=mesh['shot'=4,'gx'=4,'gy'=2] {'shot','gx','gy'}, use_global_device_ids=true, to_apply=%region_1.2 | all-reduce | flops 12288 | bytes 98304 | tf_op jit(solution)/shard_map/psum | solution.py:238
  (174 shorter events, 58.1 us)
Async XLA Ops:
  7.2 28.1 %copy-start = (f32[64,128]{1,0:T(8,128)S(1)}, f32[64,128]{1,0:T(8,128)}, u32[]{:S(2)}) copy-start(f32[64,128]{1,0:T(8,128)} %param.13) | copy-start | bytes 98308
  7.2 26.5 %copy-start.10 = (f32[1,3,24,32,128]{4,3,2,1,0:T(8,128)S(1)}, f32[1,3,24,32,128]{4,3,2,1,0:T(8,128)}, u32[]{:S(2)}) copy-start(f32[1,3,24,32,128]{4,3,2,1,0:T(8,128)} %param.17) | copy-start | bytes 3538948
  7.2 27.5 %copy-start.14 = (f32[8,6,512]{2,0,1:T(8,128)S(1)}, f32[8,6,512]{2,0,1:T(8,128)}, u32[]{:S(2)}) copy-start(f32[8,6,512]{2,0,1:T(8,128)} %param.11) | copy-start | bytes 294916
  7.2 27.6 %copy-start.12 = (f32[64,64]{1,0:T(8,128)S(1)}, f32[64,64]{1,0:T(8,128)}, u32[]{:S(2)}) copy-start(f32[64,64]{1,0:T(8,128)} %param.12) | copy-start | bytes 49156
  7.2 278.8 %reduce-scatter.4.cloned.1.call-start = ((), (), s32[]{:S(2)}) async-start(), calls=%async_computation.1 | async-start | bytes 983040
  8.9 147.3 %collective-permute-start = (f32[4,32,128]{2,1,0:T(8,128)}, f32[4,32,128]{2,1,0:T(8,128)}, u32[]{:S(2)}, u32[]{:S(2)}) collective-permute-start(f32[4,32,128]{2,1,0:T(8,128)} %get-tuple-element.116), channel_id=1, source_target_pairs={{0,2},{2,4},{4,6},{1,3},{3,5},{5,7},{8,10},{10,12},{12,14},{9,11},... | collective-permute-start | bytes 196616 | tf_op jit(solution)/shard_map/while/body/eval_jaxpr/ppermute | solution.py:16
  16.1 112.9 %collective-permute-start.10 = (f32[24,8,128]{2,1,0:T(8,128)}, f32[24,8,128]{2,1,0:T(8,128)}, u32[]{:S(2)}, u32[]{:S(2)}) collective-permute-start(f32[24,8,128]{2,1,0:T(8,128)} %get-tuple-element.146), channel_id=1, source_target_pairs={{0,1},{2,3},{4,5},{6,7},{8,9},{10,11},{12,13},{14,15},{16,17},{18,... | collective-permute-start | bytes 294920 | tf_op jit(solution)/shard_map/while/body/eval_jaxpr/ppermute | solution.py:16
  20.1 114.1 %collective-permute-start.11 = (f32[24,8,128]{2,1,0:T(8,128)}, f32[24,8,128]{2,1,0:T(8,128)}, u32[]{:S(2)}, u32[]{:S(2)}) collective-permute-start(f32[24,8,128]{2,1,0:T(8,128)} %get-tuple-element.147), channel_id=1, source_target_pairs={{1,0},{3,2},{5,4},{7,6},{9,8},{11,10},{13,12},{15,14},{17,16},{19,... | collective-permute-start | bytes 294920 | tf_op jit(solution)/shard_map/while/body/eval_jaxpr/ppermute | solution.py:19
  24.0 112.5 %collective-permute-start.6 = (f32[24,4,128]{2,1,0:T(4,128)}, f32[24,4,128]{2,1,0:T(4,128)S(1)}, u32[]{:S(2)}, u32[]{:S(2)}) collective-permute-start(f32[24,4,128]{2,1,0:T(4,128)} %get-tuple-element.152), channel_id=1, source_target_pairs={{0,1},{2,3},{4,5},{6,7},{8,9},{10,11},{12,13},{14,15},{16,17},{18,... | collective-permute-start | bytes 147464 | tf_op jit(solution)/shard_map/while/body/eval_jaxpr/ppermute | solution.py:16
  29.2 108.8 %collective-permute-start.7 = (f32[24,4,128]{2,1,0:T(4,128)}, f32[24,4,128]{2,1,0:T(4,128)}, u32[]{:S(2)}, u32[]{:S(2)}) collective-permute-start(f32[24,4,128]{2,1,0:T(4,128)} %get-tuple-element.153), channel_id=1, source_target_pairs={{1,0},{3,2},{5,4},{7,6},{9,8},{11,10},{13,12},{15,14},{17,16},{19,... | collective-permute-start | bytes 147464 | tf_op jit(solution)/shard_map/while/body/eval_jaxpr/ppermute | solution.py:19
  87.7 2.0 copy-start.22
  87.7 3.9 %copy-start.23 = (f32[3,1]{0,1:T(1,128)S(1)}, f32[3,1]{0,1:T(1,128)}, u32[]{:S(2)}) copy-start(f32[3,1]{0,1:T(1,128)} %param.19) | copy-start | bytes 40
  87.7 4.5 %copy-start.20 = (s32[1,3,2048]{2,0,1:T(1,128)S(1)}, s32[1,3,2048]{2,0,1:T(1,128)}, u32[]{:S(2)}) copy-start(s32[1,3,2048]{2,0,1:T(1,128)} %param.20) | copy-start | bytes 73732
  87.7 4.5 %copy-start.21 = (f32[1,3,2048]{2,0,1:T(1,128)S(1)}, f32[1,3,2048]{2,0,1:T(1,128)}, u32[]{:S(2)}) copy-start(f32[1,3,2048]{2,0,1:T(1,128)} %param.21) | copy-start | bytes 73732
  121.4 5.2 %copy-start.1 = (f32[1,24,32,128]{3,2,1,0:T(8,128)S(1)}, f32[1,24,32,128]{3,2,1,0:T(8,128)}, u32[]{:S(2)}) copy-start(f32[1,24,32,128]{3,2,1,0:T(8,128)} %param.14) | copy-start | bytes 1179652
  124.0 18.6 %copy-start.13 = (f32[8,32,128]{2,1,0:T(8,128)S(1)}, f32[8,32,128]{2,1,0:T(8,128)}, u32[]{:S(2)}) copy-start(f32[8,32,128]{2,1,0:T(8,128)} %get-tuple-element.144) | copy-start | bytes 393220
  129.1 13.5 %collective-permute-start.8 = (f32[24,4,128]{2,1,0:T(4,128)S(1)}, f32[24,4,128]{2,1,0:T(4,128)S(1)}, u32[]{:S(2)}, u32[]{:S(2)}) collective-permute-start(f32[24,4,128]{2,1,0:T(4,128)S(1)} %get-tuple-element.148), channel_id=1, source_target_pairs={{0,1},{2,3},{4,5},{6,7},{8,9},{10,11},{12,13},{14,15},{16,17},{18,... | collective-permute-start | bytes 147464 | tf_op jit(solution)/shard_map/ppermute | solution.py:16
  134.2 11.2 %collective-permute-start.9 = (f32[24,4,128]{2,1,0:T(4,128)S(1)}, f32[24,4,128]{2,1,0:T(4,128)S(1)}, u32[]{:S(2)}, u32[]{:S(2)}) collective-permute-start(f32[24,4,128]{2,1,0:T(4,128)S(1)} %get-tuple-element.149), channel_id=1, source_target_pairs={{1,0},{3,2},{5,4},{7,6},{9,8},{11,10},{13,12},{15,14},{17,16},{19,... | collective-permute-start | bytes 147464 | tf_op jit(solution)/shard_map/ppermute | solution.py:19
  136.5 11.9 %copy-start.16 = (f32[1,4,32,128]{3,2,1,0:T(8,128)S(1)}, f32[1,4,32,128]{3,2,1,0:T(8,128)}, u32[]{:S(2)}) copy-start(f32[1,4,32,128]{3,2,1,0:T(8,128)} %copy.83) | copy-start | bytes 196612
  136.5 16.1 %copy-start.15 = (f32[1,4,32,128]{3,2,1,0:T(8,128)S(1)}, f32[1,4,32,128]{3,2,1,0:T(8,128)}, u32[]{:S(2)}) copy-start(f32[1,4,32,128]{3,2,1,0:T(8,128)} %copy.81) | copy-start | bytes 196612
  136.5 21.0 %collective-permute-start.1 = (f32[4,32,128]{2,1,0:T(8,128)}, f32[4,32,128]{2,1,0:T(8,128)S(1)}, u32[]{:S(2)}, u32[]{:S(2)}) collective-permute-start(f32[4,32,128]{2,1,0:T(8,128)} %get-tuple-element.117), channel_id=1, source_target_pairs={{2,0},{4,2},{6,4},{3,1},{5,3},{7,5},{10,8},{12,10},{14,12},{11,9},... | collective-permute-start | bytes 196616 | tf_op jit(solution)/shard_map/while/body/eval_jaxpr/ppermute | solution.py:19
  138.0 87.4 %collective-permute-start.20 = (f32[4,32,128]{2,1,0:T(8,128)}, f32[4,32,128]{2,1,0:T(8,128)S(1)}, u32[]{:S(2)}, u32[]{:S(2)}) collective-permute-start(f32[4,32,128]{2,1,0:T(8,128)} %get-tuple-element.112), channel_id=1, source_target_pairs={{0,2},{2,4},{4,6},{1,3},{3,5},{5,7},{8,10},{10,12},{12,14},{9,11},... | collective-permute-start | bytes 196616 | tf_op jit(solution)/shard_map/while/body/eval_jaxpr/ppermute | solution.py:16
  142.6 5.8 %collective-permute-start.4 = (f32[8,32,128]{2,1,0:T(8,128)S(1)}, f32[8,32,128]{2,1,0:T(8,128)S(1)}, u32[]{:S(2)}, u32[]{:S(2)}) collective-permute-start(f32[8,32,128]{2,1,0:T(8,128)S(1)} %copy-done.13), channel_id=1, source_target_pairs={{0,2},{2,4},{4,6},{1,3},{3,5},{5,7},{8,10},{10,12},{12,14},{9,11},... | collective-permute-start | bytes 393224 | tf_op jit(solution)/shard_map/while/body/eval_jaxpr/ppermute | solution.py:16
  145.4 10.8 %copy-start.17 = (f32[4,32,128]{2,1,0:T(8,128)S(1)}, f32[4,32,128]{2,1,0:T(8,128)}, u32[]{:S(2)}) copy-start(f32[4,32,128]{2,1,0:T(8,128)} %get-tuple-element.113) | copy-start | bytes 196612
  145.4 12.1 %copy-start.19 = (f32[24,4,128]{2,1,0:T(4,128)S(1)}, f32[24,4,128]{2,1,0:T(4,128)}, u32[]{:S(2)}) copy-start(f32[24,4,128]{2,1,0:T(4,128)} %get-tuple-element.132) | copy-start | bytes 147460
  145.4 16.8 %copy-start.7 = (f32[24,32,128]{2,1,0:T(8,128)S(1)}, f32[24,32,128]{2,1,0:T(8,128)}, u32[]{:S(2)}) copy-start(f32[24,32,128]{2,1,0:T(8,128)} %get-tuple-element.118) | copy-start | bytes 1179652
  145.5 7.2 %collective-permute-start.5 = (f32[8,32,128]{2,1,0:T(8,128)}, f32[8,32,128]{2,1,0:T(8,128)S(1)}, u32[]{:S(2)}, u32[]{:S(2)}) collective-permute-start(f32[8,32,128]{2,1,0:T(8,128)} %get-tuple-element.145), channel_id=1, source_target_pairs={{2,0},{4,2},{6,4},{3,1},{5,3},{7,5},{10,8},{12,10},{14,12},{11,9},... | collective-permute-start | bytes 393224 | tf_op jit(solution)/shard_map/while/body/eval_jaxpr/ppermute | solution.py:19
  148.4 13.9 %collective-permute-start.3 = (f32[4,32,128]{2,1,0:T(8,128)S(1)}, f32[4,32,128]{2,1,0:T(8,128)S(1)}, u32[]{:S(2)}, u32[]{:S(2)}) collective-permute-start(f32[4,32,128]{2,1,0:T(8,128)S(1)} %bitcast.176), channel_id=1, source_target_pairs={{2,0},{4,2},{6,4},{3,1},{5,3},{7,5},{10,8},{12,10},{14,12},{11,9},... | collective-permute-start | bytes 196616 | tf_op jit(solution)/shard_map/ppermute | solution.py:19
  152.7 9.6 %collective-permute-start.2 = (f32[4,32,128]{2,1,0:T(8,128)S(1)}, f32[4,32,128]{2,1,0:T(8,128)S(1)}, u32[]{:S(2)}, u32[]{:S(2)}) collective-permute-start(f32[4,32,128]{2,1,0:T(8,128)S(1)} %bitcast.175), channel_id=1, source_target_pairs={{0,2},{2,4},{4,6},{1,3},{3,5},{5,7},{8,10},{10,12},{12,14},{9,11},... | collective-permute-start | bytes 196616 | tf_op jit(solution)/shard_map/ppermute | solution.py:16
  156.2 69.2 %collective-permute-start.21 = (f32[4,32,128]{2,1,0:T(8,128)S(1)}, f32[4,32,128]{2,1,0:T(8,128)S(1)}, u32[]{:S(2)}, u32[]{:S(2)}) collective-permute-start(f32[4,32,128]{2,1,0:T(8,128)S(1)} %copy-done.17), channel_id=1, source_target_pairs={{2,0},{4,2},{6,4},{3,1},{5,3},{7,5},{10,8},{12,10},{14,12},{11,9},... | collective-permute-start | bytes 196616 | tf_op jit(solution)/shard_map/while/body/eval_jaxpr/ppermute | solution.py:19
  157.5 60.8 %collective-permute-start.24 = (f32[24,4,128]{2,1,0:T(4,128)S(1)}, f32[24,4,128]{2,1,0:T(4,128)S(1)}, u32[]{:S(2)}, u32[]{:S(2)}) collective-permute-start(f32[24,4,128]{2,1,0:T(4,128)S(1)} %copy-done.19), channel_id=1, source_target_pairs={{0,1},{2,3},{4,5},{6,7},{8,9},{10,11},{12,13},{14,15},{16,17},{18,... | collective-permute-start | bytes 147464 | tf_op jit(solution)/shard_map/while/body/eval_jaxpr/ppermute | solution.py:16
  165.7 3.5 collective-permute-start.14
  167.0 6.7 %collective-permute-start.15 = (f32[24,8,128]{2,1,0:T(8,128)S(1)}, f32[24,8,128]{2,1,0:T(8,128)S(1)}, u32[]{:S(2)}, u32[]{:S(2)}) collective-permute-start(f32[24,8,128]{2,1,0:T(8,128)S(1)} %get-tuple-element.143), channel_id=1, source_target_pairs={{1,0},{3,2},{5,4},{7,6},{9,8},{11,10},{13,12},{15,14},{17,16},{19,... | collective-permute-start | bytes 294920 | tf_op jit(solution)/shard_map/while/body/eval_jaxpr/ppermute | solution.py:19
  169.2 7.0 %collective-permute-start.12 = (f32[8,32,128]{2,1,0:T(8,128)S(1)}, f32[8,32,128]{2,1,0:T(8,128)S(1)}, u32[]{:S(2)}, u32[]{:S(2)}) collective-permute-start(f32[8,32,128]{2,1,0:T(8,128)S(1)} %get-tuple-element.140), channel_id=1, source_target_pairs={{0,2},{2,4},{4,6},{1,3},{3,5},{5,7},{8,10},{10,12},{12,14},{9,11},... | collective-permute-start | bytes 393224 | tf_op jit(solution)/shard_map/while/body/eval_jaxpr/ppermute | solution.py:16
  173.8 7.2 %collective-permute-start.13 = (f32[8,32,128]{2,1,0:T(8,128)S(1)}, f32[8,32,128]{2,1,0:T(8,128)S(1)}, u32[]{:S(2)}, u32[]{:S(2)}) collective-permute-start(f32[8,32,128]{2,1,0:T(8,128)S(1)} %get-tuple-element.141), channel_id=1, source_target_pairs={{2,0},{4,2},{6,4},{3,1},{5,3},{7,5},{10,8},{12,10},{14,12},{11,9},... | collective-permute-start | bytes 393224 | tf_op jit(solution)/shard_map/while/body/eval_jaxpr/ppermute | solution.py:19
  183.6 6.1 %collective-permute-start.18 = (f32[24,8,128]{2,1,0:T(8,128)S(1)}, f32[24,8,128]{2,1,0:T(8,128)S(1)}, u32[]{:S(2)}, u32[]{:S(2)}) collective-permute-start(f32[24,8,128]{2,1,0:T(8,128)S(1)} %get-tuple-element.138), channel_id=1, source_target_pairs={{0,1},{2,3},{4,5},{6,7},{8,9},{10,11},{12,13},{14,15},{16,17},{18,... | collective-permute-start | bytes 294920 | tf_op jit(solution)/shard_map/while/body/eval_jaxpr/ppermute | solution.py:16
  187.5 6.5 %collective-permute-start.19 = (f32[24,8,128]{2,1,0:T(8,128)S(1)}, f32[24,8,128]{2,1,0:T(8,128)S(1)}, u32[]{:S(2)}, u32[]{:S(2)}) collective-permute-start(f32[24,8,128]{2,1,0:T(8,128)S(1)} %get-tuple-element.139), channel_id=1, source_target_pairs={{1,0},{3,2},{5,4},{7,6},{9,8},{11,10},{13,12},{15,14},{17,16},{19,... | collective-permute-start | bytes 294920 | tf_op jit(solution)/shard_map/while/body/eval_jaxpr/ppermute | solution.py:19
  189.7 6.2 %collective-permute-start.16 = (f32[8,32,128]{2,1,0:T(8,128)S(1)}, f32[8,32,128]{2,1,0:T(8,128)S(1)}, u32[]{:S(2)}, u32[]{:S(2)}) collective-permute-start(f32[8,32,128]{2,1,0:T(8,128)S(1)} %get-tuple-element.136), channel_id=1, source_target_pairs={{0,2},{2,4},{4,6},{1,3},{3,5},{5,7},{8,10},{10,12},{12,14},{9,11},... | collective-permute-start | bytes 393224 | tf_op jit(solution)/shard_map/while/body/eval_jaxpr/ppermute | solution.py:16
  194.0 6.8 %collective-permute-start.17 = (f32[8,32,128]{2,1,0:T(8,128)S(1)}, f32[8,32,128]{2,1,0:T(8,128)S(1)}, u32[]{:S(2)}, u32[]{:S(2)}) collective-permute-start(f32[8,32,128]{2,1,0:T(8,128)S(1)} %get-tuple-element.137), channel_id=1, source_target_pairs={{2,0},{4,2},{6,4},{3,1},{5,3},{7,5},{10,8},{12,10},{14,12},{11,9},... | collective-permute-start | bytes 393224 | tf_op jit(solution)/shard_map/while/body/eval_jaxpr/ppermute | solution.py:19
  200.9 1.0 copy-start.8
  200.9 1.1 copy-start.9
  200.9 1.2 copy-start.11
  202.2 8.3 %copy-start.18 = (f32[24,4,128]{2,1,0:T(4,128)S(1)}, f32[24,4,128]{2,1,0:T(4,128)}, u32[]{:S(2)}) copy-start(f32[24,4,128]{2,1,0:T(4,128)} %get-tuple-element.133) | copy-start | bytes 147460
  203.7 16.1 %copy-start.2 = (f32[24,32,128]{2,1,0:T(8,128)S(1)}, f32[24,32,128]{2,1,0:T(8,128)}, u32[]{:S(2)}) copy-start(f32[24,32,128]{2,1,0:T(8,128)} %get-tuple-element.115) | copy-start | bytes 1179652
  205.6 4.9 %collective-permute-start.26 = (f32[24,8,128]{2,1,0:T(8,128)S(1)}, f32[24,8,128]{2,1,0:T(8,128)S(1)}, u32[]{:S(2)}, u32[]{:S(2)}) collective-permute-start(f32[24,8,128]{2,1,0:T(8,128)S(1)} %get-tuple-element.134), channel_id=1, source_target_pairs={{0,1},{2,3},{4,5},{6,7},{8,9},{10,11},{12,13},{14,15},{16,17},{18,... | collective-permute-start | bytes 294920 | tf_op jit(solution)/shard_map/while/body/eval_jaxpr/ppermute | solution.py:16
  208.3 6.5 %collective-permute-start.27 = (f32[24,8,128]{2,1,0:T(8,128)S(1)}, f32[24,8,128]{2,1,0:T(8,128)S(1)}, u32[]{:S(2)}, u32[]{:S(2)}) collective-permute-start(f32[24,8,128]{2,1,0:T(8,128)S(1)} %get-tuple-element.135), channel_id=1, source_target_pairs={{1,0},{3,2},{5,4},{7,6},{9,8},{11,10},{13,12},{15,14},{17,16},{19,... | collective-permute-start | bytes 294920 | tf_op jit(solution)/shard_map/while/body/eval_jaxpr/ppermute | solution.py:19
  210.5 9.3 %collective-permute-start.25 = (f32[24,4,128]{2,1,0:T(4,128)S(1)}, f32[24,4,128]{2,1,0:T(4,128)S(1)}, u32[]{:S(2)}, u32[]{:S(2)}) collective-permute-start(f32[24,4,128]{2,1,0:T(4,128)S(1)} %copy-done.18), channel_id=1, source_target_pairs={{1,0},{3,2},{5,4},{7,6},{9,8},{11,10},{13,12},{15,14},{17,16},{19,... | collective-permute-start | bytes 147464 | tf_op jit(solution)/shard_map/while/body/eval_jaxpr/ppermute | solution.py:19
  214.8 6.0 %collective-permute-start.22 = (f32[8,32,128]{2,1,0:T(8,128)S(1)}, f32[8,32,128]{2,1,0:T(8,128)S(1)}, u32[]{:S(2)}, u32[]{:S(2)}) collective-permute-start(f32[8,32,128]{2,1,0:T(8,128)S(1)} %get-tuple-element.130), channel_id=1, source_target_pairs={{0,2},{2,4},{4,6},{1,3},{3,5},{5,7},{8,10},{10,12},{12,14},{9,11},... | collective-permute-start | bytes 393224 | tf_op jit(solution)/shard_map/while/body/eval_jaxpr/ppermute | solution.py:16
  218.3 7.1 %copy-start.6 = (f32[24,32,128]{2,1,0:T(8,128)S(1)}, f32[24,32,128]{2,1,0:T(8,128)}, u32[]{:S(2)}) copy-start(f32[24,32,128]{2,1,0:T(8,128)} %get-tuple-element.114) | copy-start | bytes 1179652
  218.3 7.0 %collective-permute-start.23 = (f32[8,32,128]{2,1,0:T(8,128)S(1)}, f32[8,32,128]{2,1,0:T(8,128)S(1)}, u32[]{:S(2)}, u32[]{:S(2)}) collective-permute-start(f32[8,32,128]{2,1,0:T(8,128)S(1)} %get-tuple-element.131), channel_id=1, source_target_pairs={{2,0},{4,2},{6,4},{3,1},{5,3},{7,5},{10,8},{12,10},{14,12},{11,9},... | collective-permute-start | bytes 393224 | tf_op jit(solution)/shard_map/while/body/eval_jaxpr/ppermute | solution.py:19
  225.4 1.0 copy-start.4
  225.4 1.1 copy-start.5
  228.1 6.1 %collective-permute-start.30 = (f32[24,8,128]{2,1,0:T(8,128)S(1)}, f32[24,8,128]{2,1,0:T(8,128)S(1)}, u32[]{:S(2)}, u32[]{:S(2)}) collective-permute-start(f32[24,8,128]{2,1,0:T(8,128)S(1)} %get-tuple-element.128), channel_id=1, source_target_pairs={{0,1},{2,3},{4,5},{6,7},{8,9},{10,11},{12,13},{14,15},{16,17},{18,... | collective-permute-start | bytes 294920 | tf_op jit(solution)/shard_map/while/body/eval_jaxpr/ppermute | solution.py:16
  229.7 6.5 %collective-permute-start.31 = (f32[24,8,128]{2,1,0:T(8,128)S(1)}, f32[24,8,128]{2,1,0:T(8,128)S(1)}, u32[]{:S(2)}, u32[]{:S(2)}) collective-permute-start(f32[24,8,128]{2,1,0:T(8,128)S(1)} %get-tuple-element.129), channel_id=1, source_target_pairs={{1,0},{3,2},{5,4},{7,6},{9,8},{11,10},{13,12},{15,14},{17,16},{19,... | collective-permute-start | bytes 294920 | tf_op jit(solution)/shard_map/while/body/eval_jaxpr/ppermute | solution.py:19
  231.0 5.7 %collective-permute-start.28 = (f32[8,32,128]{2,1,0:T(8,128)S(1)}, f32[8,32,128]{2,1,0:T(8,128)S(1)}, u32[]{:S(2)}, u32[]{:S(2)}) collective-permute-start(f32[8,32,128]{2,1,0:T(8,128)S(1)} %get-tuple-element.126), channel_id=1, source_target_pairs={{0,2},{2,4},{4,6},{1,3},{3,5},{5,7},{8,10},{10,12},{12,14},{9,11},... | collective-permute-start | bytes 393224 | tf_op jit(solution)/shard_map/while/body/eval_jaxpr/ppermute | solution.py:16
  232.9 6.9 %collective-permute-start.29 = (f32[8,32,128]{2,1,0:T(8,128)S(1)}, f32[8,32,128]{2,1,0:T(8,128)S(1)}, u32[]{:S(2)}, u32[]{:S(2)}) collective-permute-start(f32[8,32,128]{2,1,0:T(8,128)S(1)} %get-tuple-element.127), channel_id=1, source_target_pairs={{2,0},{4,2},{6,4},{3,1},{5,3},{7,5},{10,8},{12,10},{14,12},{11,9},... | collective-permute-start | bytes 393224 | tf_op jit(solution)/shard_map/while/body/eval_jaxpr/ppermute | solution.py:19
  239.8 1.0 copy-start.3
  241.7 9.3 %collective-permute-start.34 = (f32[24,8,128]{2,1,0:T(8,128)S(1)}, f32[24,8,128]{2,1,0:T(8,128)S(1)}, u32[]{:S(2)}, u32[]{:S(2)}) collective-permute-start(f32[24,8,128]{2,1,0:T(8,128)S(1)} %get-tuple-element.124), channel_id=1, source_target_pairs={{0,1},{2,3},{4,5},{6,7},{8,9},{10,11},{12,13},{14,15},{16,17},{18,... | collective-permute-start | bytes 294920 | tf_op jit(solution)/shard_map/while/body/eval_jaxpr/ppermute | solution.py:16
  246.2 6.5 %collective-permute-start.35 = (f32[24,8,128]{2,1,0:T(8,128)S(1)}, f32[24,8,128]{2,1,0:T(8,128)S(1)}, u32[]{:S(2)}, u32[]{:S(2)}) collective-permute-start(f32[24,8,128]{2,1,0:T(8,128)S(1)} %get-tuple-element.125), channel_id=1, source_target_pairs={{1,0},{3,2},{5,4},{7,6},{9,8},{11,10},{13,12},{15,14},{17,16},{19,... | collective-permute-start | bytes 294920 | tf_op jit(solution)/shard_map/while/body/eval_jaxpr/ppermute | solution.py:19
  247.6 5.7 %collective-permute-start.32 = (f32[8,32,128]{2,1,0:T(8,128)S(1)}, f32[8,32,128]{2,1,0:T(8,128)S(1)}, u32[]{:S(2)}, u32[]{:S(2)}) collective-permute-start(f32[8,32,128]{2,1,0:T(8,128)S(1)} %get-tuple-element.122), channel_id=1, source_target_pairs={{0,2},{2,4},{4,6},{1,3},{3,5},{5,7},{8,10},{10,12},{12,14},{9,11},... | collective-permute-start | bytes 393224 | tf_op jit(solution)/shard_map/while/body/eval_jaxpr/ppermute | solution.py:16
  249.5 6.9 %collective-permute-start.33 = (f32[8,32,128]{2,1,0:T(8,128)S(1)}, f32[8,32,128]{2,1,0:T(8,128)S(1)}, u32[]{:S(2)}, u32[]{:S(2)}) collective-permute-start(f32[8,32,128]{2,1,0:T(8,128)S(1)} %get-tuple-element.123), channel_id=1, source_target_pairs={{2,0},{4,2},{6,4},{3,1},{5,3},{7,5},{10,8},{12,10},{14,12},{11,9},... | collective-permute-start | bytes 393224 | tf_op jit(solution)/shard_map/while/body/eval_jaxpr/ppermute | solution.py:19
Sparse Core Ops, SparseCore 0:
  264.3 21.5 reduce-scatter.3
where the time goes:
time: 377 us; the launch traced here: 370 us
  starting transfers between devices  87.9 us (23%)
  local copies, waits for them, and re-layouts  87 us (23%)
  blocking collectives  62.2 us (16%)
  waiting for transfers between devices  57.2 us (15%)
  other arithmetic  51.9 us (14%)
  between operations  16.7 us (4%)
  matrix products  7.16 us (2%)
    ppermute x18, starting transfers between devices, with_halo(): lax.ppermute(lax.slice_in_dim(block, block.shape[dim] - width, None, axis...  64.1 us
    psum x1, blocking collectives, body(): lax.psum((grad_first, grad_second), ('shot', 'gx', 'gy'))  40.3 us
    ppermute x18, waiting for transfers between devices, with_halo(): lax.ppermute(lax.slice_in_dim(block, 0, width, axis=dim), axis, backward)  31.8 us
    ppermute x18, starting transfers between devices, with_halo(): lax.ppermute(lax.slice_in_dim(block, 0, width, axis=dim), axis, backward)  23.8 us
    all_gather x1, blocking collectives, body(): lax.all_gather(jnp.stack([slab_mod, slab_buoy]), 'shot', axis=3, tiled=True)  21.9 us
    unnamed x2, waiting for transfers between devices  21.8 us
    div x4, local copies, waits for them, and re-layouts, materials(): wave_speed = 0.15 + 0.25 * jax.nn.sigmoid(fine_out[0])  17.6 us
    transpose x1, local copies, waits for them, and re-layouts, decoder_grads(): grad_out = grad_fine.reshape(2, size_x // 4, 4, size_y // 4, 4, size_z //...  17 us
  transfers between devices with their start and end apart: 37, of which 16 were waited for; matrix products, arithmetic and copies ran while one was open for 25% of the time, Pallas kernels for 0%

commit v1 on v0

--- a/solution.py
+++ b/solution.py
@@ -1,3 +1,4 @@
+import functools
 import jax
 import jax.numpy as jnp
 from jax import lax
@@ -6,6 +7,27 @@
 CH = 64
 STEPS = 3
 coeffs = (1225.0 / 1024.0, -245.0 / 3072.0, 49.0 / 5120.0, -5.0 / 7168.0)
+
+
+def _recover_rounds(xx, lane_axis, where_dim):
+    wide_out, carry_out, far_arr = (
+        lax.axis_size(lane_axis),
+        lax.axis_index(lane_axis),
+        xx.shape[where_dim],
+    )
+    x_new, view_out = (xx, 1)
+    while view_out < wide_out:
+        store = []
+        p = 0
+        while p < wide_out:
+            store.append((p, (p - view_out) % wide_out))
+            p = p + 1
+        x_new = jnp.concatenate([x_new, lax.ppermute(x_new, lane_axis, store)], axis=where_dim)
+        view_out = 2 * view_out
+    return jnp.roll(x_new, carry_out * far_arr, axis=where_dim)
+
+
+open_gates_here = functools.partial(_recover_rounds, lane_axis="shot", where_dim=3)
 
 
 def with_halo(block, sides, width):
@@ -170,7 +192,7 @@
     anchor_y = lax.axis_index("gy") * size_y
     flattened, hidden, fine_out = decode(latent, w_first, w_second)
     slab_mod, slab_buoy = materials(fine_out)
-    stacked = lax.all_gather(jnp.stack([slab_mod, slab_buoy]), "shot", axis=3, tiled=True)
+    stacked = open_gates_here(jnp.stack([slab_mod, slab_buoy]))
     modulus, buoyancy = (stacked[0], stacked[1])
     buoy_x = rim_x(buoyancy)
     buoy_y = rim_y(buoyancy)

time: 377 us -> 359 us (0.952)
  blocking collectives: 62.2 us -> 40.3 us
  starting transfers between devices: 87.9 us -> 96.4 us
  local copies, waits for them, and re-layouts: 87 us -> 78.6 us
    all_gather x1 -> x0, blocking collectives: 21.9 us -> none  [body(): lax.all_gather(jnp.stack([slab_mod, slab_buoy]), 'shot', axis=3, tiled=True)]
    ppermute x18, starting transfers between devices: 64.1 us -> 70.7 us  [with_halo(): lax.ppermute(lax.slice_in_dim(block, block.shape[dim] - width, None, axis...]
    unnamed x60, local copies, waits for them, and re-layouts: 16.4 us -> 10.7 us
    ppermute x18, waiting for transfers between devices: 31.8 us -> 27.3 us  [with_halo(): lax.ppermute(lax.slice_in_dim(block, 0, width, axis=dim), axis, backward)]
    concatenate x0 -> x1, local copies, waits for them, and re-layouts: none -> 4.09 us  [_recover_rounds(): return jnp.roll(x_new, carry_out * far_arr, axis=where_dim)]
  transfers between devices with their start and end apart: 37 -> 39, of which waited for: 16 -> 17; matrix products, arithmetic and copies ran while one was open for 25% -> 26% of each run, Pallas kernels for 0% -> 0%
where the time goes in v1:
time: 359 us; the launch traced here: 352 us
  starting transfers between devices  96.4 us (27%)
  local copies, waits for them, and re-layouts  78.6 us (22%)
  waiting for transfers between devices  57.5 us (16%)
  other arithmetic  54.3 us (15%)
  blocking collectives  40.3 us (11%)
  between operations  16.7 us (5%)
  matrix products  7.92 us (2%)
    ppermute x18, starting transfers between devices, with_halo(): lax.ppermute(lax.slice_in_dim(block, block.shape[dim] - width, None, axis...  70.7 us
    psum x1, blocking collectives, body(): lax.psum((grad_first, grad_second), ('shot', 'gx', 'gy'))  40.3 us
    ppermute x18, waiting for transfers between devices, with_halo(): lax.ppermute(lax.slice_in_dim(block, 0, width, axis=dim), axis, backward)  27.3 us
    ppermute x18, starting transfers between devices, with_halo(): lax.ppermute(lax.slice_in_dim(block, 0, width, axis=dim), axis, backward)  23.6 us
    unnamed x2, waiting for transfers between devices  22.8 us
    transpose x1, local copies, waits for them, and re-layouts, decoder_grads(): grad_out = grad_fine.reshape(2, size_x // 4, 4, size_y // 4, 4, size_z //...  17 us
    div x4, local copies, waits for them, and re-layouts, materials(): wave_speed = 0.15 + 0.25 * jax.nn.sigmoid(fine_out[0])  14.6 us
    add x1, other arithmetic, receiver_fields(): planes[:, :, 1 + 2 * m] + planes[:, :, 2 + 2 * m]  12.5 us
  transfers between devices with their start and end apart: 39, of which 17 were waited for; matrix products, arithmetic and copies ran while one was open for 26% of the time, Pallas kernels for 0%

profile of v1, /device:TPU:0, one launch (start us, length us, event | category | flops | bytes accessed | tf_op | source)
XLA Modules:
  0.0 351.8 jit_solution(1062184977956135061)
XLA Ops:
  7.2 1.6 fusion.399
  8.9 5.5 %collective-permute-start.12 = (f32[24,8,128]{2,1,0:T(8,128)}, f32[24,8,128]{2,1,0:T(8,128)}, u32[]{:S(2)}, u32[]{:S(2)}) collective-permute-start(f32[24,8,128]{2,1,0:T(8,128)} %get-tuple-element.145), channel_id=1, source_target_pairs={{0,1},{2,3},{4,5},{6,7},{8,9},{10,11},{12,13},{14,15},{16,17},{18,... | collective-permute-start | bytes 294920 | tf_op jit(solution)/shard_map/while/body/eval_jaxpr/ppermute | solution.py:38
  15.6 1.7 slice_bitcast_fusion.5
  17.3 4.1 %collective-permute-start.6 = (f32[8,32,128]{2,1,0:T(8,128)}, f32[8,32,128]{2,1,0:T(8,128)}, u32[]{:S(2)}, u32[]{:S(2)}) collective-permute-start(f32[8,32,128]{2,1,0:T(8,128)} %get-tuple-element.143), channel_id=1, source_target_pairs={{0,2},{2,4},{4,6},{1,3},{3,5},{5,7},{8,10},{10,12},{12,14},{9,11},... | collective-permute-start | bytes 393224 | tf_op jit(solution)/shard_map/while/body/eval_jaxpr/ppermute | solution.py:38
  25.4 3.1 reshape.228
  28.5 3.4 copy.53
  31.9 2.4 fusion.4
  34.3 5.7 %copy.55 = f32[1,6,4,8,4,8,4]{6,5,4,3,2,1,0:T(8,128)S(1)} copy(f32[1,6,4,8,4,8,4]{5,3,6,4,2,1,0:T(8,128)} %get-tuple-element.105) | data formatting | bytes 196608 | tf_op jit(solution)/shard_map/div | solution.py:119
  40.0 1.6 div.74
  41.6 5.7 %copy.54 = f32[1,6,4,8,4,8,4]{6,5,4,3,2,1,0:T(8,128)S(1)} copy(f32[1,6,4,8,4,8,4]{5,3,6,4,2,1,0:T(8,128)} %get-tuple-element.106) | data formatting | bytes 196608 | tf_op jit(solution)/shard_map/div | solution.py:119
  47.4 1.6 div.72
  51.3 1.5 slice_bitcast_fusion.9
  52.8 1.9 slice_bitcast_fusion.3
  54.7 1.7 slice_bitcast_fusion.7
  56.4 1.9 slice_bitcast_fusion.1
  67.6 5.0 %fusion = f32[768,896]{1,0:T(8,128)} fusion(bf16[2048,896]{1,0:T(8,128)(2,1)S(1)} %fusion.14, s32[2048]{0:T(1024)S(1)} %bitcast.156), kind=kOutput, calls=%fused_computation.2 | convolution fusion | flops 2820145152 | bytes 6430720 | tf_op jit(solution)/shard_map/while/body/eval_jaxpr/dot_general | solution.py:171
  72.6 4.1 %reshape.226 = f32[24,32,7,128]{3,2,1,0:T(8,128)} reshape(f32[768,896]{1,0:T(8,128)} %fusion) | data formatting | bytes 5505024 | tf_op jit(solution)/shard_map/while/body/eval_jaxpr/reshape | solution.py:172
  76.7 12.5 %slice_add_fusion = (f32[24,32,1,128]{3,2,1,0:T(1,128)}, f32[24,32,1,128]{3,2,1,0:T(1,128)}, f32[24,32,1,128]{3,2,1,0:T(1,128)}, f32[24,32,1,128]{3,2,1,0:T(1,12...) fusion(f32[24,32,7,128]{3,2,1,0:T(8,128)} %reshape.226), kind=kLoop, calls=%fused_computation.479 | loop fusion | flops 98304 | bytes 5111808 | tf_op jit(solution)/shard_map/while/body/eval_jaxpr/add | solution.py:173
  92.0 5.2 %collective-permute-start.2 = (f32[4,32,128]{2,1,0:T(8,128)}, f32[4,32,128]{2,1,0:T(8,128)}, u32[]{:S(2)}, u32[]{:S(2)}) collective-permute-start(f32[4,32,128]{2,1,0:T(8,128)} %get-tuple-element.115), channel_id=1, source_target_pairs={{0,2},{2,4},{4,6},{1,3},{3,5},{5,7},{8,10},{10,12},{12,14},{9,11},... | collective-permute-start | bytes 196616 | tf_op jit(solution)/shard_map/while/body/eval_jaxpr/ppermute | solution.py:38
  97.2 5.8 %collective-permute-start.8 = (f32[24,4,128]{2,1,0:T(4,128)}, f32[24,4,128]{2,1,0:T(4,128)}, u32[]{:S(2)}, u32[]{:S(2)}) collective-permute-start(f32[24,4,128]{2,1,0:T(4,128)} %get-tuple-element.151), channel_id=1, source_target_pairs={{0,1},{2,3},{4,5},{6,7},{8,9},{10,11},{12,13},{14,15},{16,17},{18,... | collective-permute-start | bytes 147464 | tf_op jit(solution)/shard_map/while/body/eval_jaxpr/ppermute | solution.py:38
  104.0 1.3 collective-permute-start.9
  106.3 3.6 %collective-permute-done.1 = f32[2,24,32,64]{3,2,1,0:T(8,128)} collective-permute-done((f32[2,24,32,64]{3,2,1,0:T(8,128)S(1)}, f32[2,24,32,64]{3,2,1,0:T(8,128)}, u32[]{:S(2)}, u32[]{:S(2)}) %collective-permute-start.1) | collective-permute-done | bytes 393248 | tf_op jit(solution)/shard_map/ppermute | solution.py:25
  109.9 4.1 %concatenate.124 = f32[2,24,32,256]{3,2,1,0:T(8,128)S(1)} concatenate(f32[2,24,32,32]{3,2,1,0:T(8,128)} %copy-done.2, f32[2,24,32,32]{3,2,1,0:T(8,128)} %copy-done.3, f32[2,24,32,64]{3,2,1,0:T(8,128)} %collective-permute-done.1, f32[2,24,32,32]{3,2,1,0:T(8,128)} %copy-done.2, f32[2,24,32,32]{3,2,1,0:T(8,128)} %copy-done.3, f32[2,24,32,64]{3,2,1,0:T(8,128)} %collective-permute-done.1), dimensions={3} | concatenate | bytes 3145728 | tf_op jit(solution)/shard_map/jit(_roll_dynamic)/concatenate | solution.py:27
  114.0 1.9 bitcast_subtract_fusion.2
  115.9 5.3 %collective-permute-start.10 = (f32[24,4,128]{2,1,0:T(4,128)S(1)}, f32[24,4,128]{2,1,0:T(4,128)S(1)}, u32[]{:S(2)}, u32[]{:S(2)}) collective-permute-start(f32[24,4,128]{2,1,0:T(4,128)S(1)} %get-tuple-element.147), channel_id=1, source_target_pairs={{0,1},{2,3},{4,5},{6,7},{8,9},{10,11},{12,13},{14,15},{16,17},{18,... | collective-permute-start | bytes 147464 | tf_op jit(solution)/shard_map/ppermute | solution.py:38
  122.7 1.3 collective-permute-start.3
  124.0 5.2 %collective-permute-start.22 = (f32[4,32,128]{2,1,0:T(8,128)}, f32[4,32,128]{2,1,0:T(8,128)S(1)}, u32[]{:S(2)}, u32[]{:S(2)}) collective-permute-start(f32[4,32,128]{2,1,0:T(8,128)} %get-tuple-element.111), channel_id=1, source_target_pairs={{0,2},{2,4},{4,6},{1,3},{3,5},{5,7},{8,10},{10,12},{12,14},{9,11},... | collective-permute-start | bytes 196616 | tf_op jit(solution)/shard_map/while/body/eval_jaxpr/ppermute | solution.py:38
  129.2 3.9 %collective-permute-start.4 = (f32[4,32,128]{2,1,0:T(8,128)S(1)}, f32[4,32,128]{2,1,0:T(8,128)S(1)}, u32[]{:S(2)}, u32[]{:S(2)}) collective-permute-start(f32[4,32,128]{2,1,0:T(8,128)S(1)} %get-tuple-element.107), channel_id=1, source_target_pairs={{0,2},{2,4},{4,6},{1,3},{3,5},{5,7},{8,10},{10,12},{12,14},{9,11},... | collective-permute-start | bytes 196616 | tf_op jit(solution)/shard_map/ppermute | solution.py:38
  134.4 1.6 maximum_subtract_fusion.1
  137.4 4.7 %collective-permute-start.26 = (f32[24,4,128]{2,1,0:T(4,128)S(1)}, f32[24,4,128]{2,1,0:T(4,128)S(1)}, u32[]{:S(2)}, u32[]{:S(2)}) collective-permute-start(f32[24,4,128]{2,1,0:T(4,128)S(1)} %copy-done.21), channel_id=1, source_target_pairs={{0,1},{2,3},{4,5},{6,7},{8,9},{10,11},{12,13},{14,15},{16,17},{18,... | collective-permute-start | bytes 147464 | tf_op jit(solution)/shard_map/while/body/eval_jaxpr/ppermute | solution.py:38
  143.3 1.6 select_add_fusion.1
  145.7 1.7 collective-permute-start.16
  147.4 1.3 collective-permute-start.17
  149.6 4.8 %collective-permute-start.14 = (f32[8,32,128]{2,1,0:T(8,128)S(1)}, f32[8,32,128]{2,1,0:T(8,128)S(1)}, u32[]{:S(2)}, u32[]{:S(2)}) collective-permute-start(f32[8,32,128]{2,1,0:T(8,128)S(1)} %get-tuple-element.139), channel_id=1, source_target_pairs={{0,2},{2,4},{4,6},{1,3},{3,5},{5,7},{8,10},{10,12},{12,14},{9,11},... | collective-permute-start | bytes 393224 | tf_op jit(solution)/shard_map/while/body/eval_jaxpr/ppermute | solution.py:38
  156.9 4.8 %collective-permute-done.15 = f32[8,32,128]{2,1,0:T(8,128)S(1)} collective-permute-done((f32[8,32,128]{2,1,0:T(8,128)S(1)}, f32[8,32,128]{2,1,0:T(8,128)S(1)}, u32[]{:S(2)}, u32[]{:S(2)}) %collective-permute-start.15) | collective-permute-done | bytes 131104 | tf_op jit(solution)/shard_map/while/body/eval_jaxpr/ppermute | solution.py:41
  162.0 1.5 select_add_fusion
  164.3 3.9 %collective-permute-start.20 = (f32[24,8,128]{2,1,0:T(8,128)S(1)}, f32[24,8,128]{2,1,0:T(8,128)S(1)}, u32[]{:S(2)}, u32[]{:S(2)}) collective-permute-start(f32[24,8,128]{2,1,0:T(8,128)S(1)} %get-tuple-element.137), channel_id=1, source_target_pairs={{0,1},{2,3},{4,5},{6,7},{8,9},{10,11},{12,13},{14,15},{16,17},{18,... | collective-permute-start | bytes 294920 | tf_op jit(solution)/shard_map/while/body/eval_jaxpr/ppermute | solution.py:38
  170.4 3.9 %collective-permute-start.18 = (f32[8,32,128]{2,1,0:T(8,128)S(1)}, f32[8,32,128]{2,1,0:T(8,128)S(1)}, u32[]{:S(2)}, u32[]{:S(2)}) collective-permute-start(f32[8,32,128]{2,1,0:T(8,128)S(1)} %get-tuple-element.135), channel_id=1, source_target_pairs={{0,2},{2,4},{4,6},{1,3},{3,5},{5,7},{8,10},{10,12},{12,14},{9,11},... | collective-permute-start | bytes 393224 | tf_op jit(solution)/shard_map/while/body/eval_jaxpr/ppermute | solution.py:38
  176.8 4.8 %collective-permute-done.19 = f32[8,32,128]{2,1,0:T(8,128)S(1)} collective-permute-done((f32[8,32,128]{2,1,0:T(8,128)S(1)}, f32[8,32,128]{2,1,0:T(8,128)S(1)}, u32[]{:S(2)}, u32[]{:S(2)}) %collective-permute-start.19) | collective-permute-done | bytes 131104 | tf_op jit(solution)/shard_map/while/body/eval_jaxpr/ppermute | solution.py:41
  183.0 1.6 fusion.369
  184.6 1.8 fusion.190
  186.4 3.9 %collective-permute-start.28 = (f32[24,8,128]{2,1,0:T(8,128)S(1)}, f32[24,8,128]{2,1,0:T(8,128)S(1)}, u32[]{:S(2)}, u32[]{:S(2)}) collective-permute-start(f32[24,8,128]{2,1,0:T(8,128)S(1)} %get-tuple-element.133), channel_id=1, source_target_pairs={{0,1},{2,3},{4,5},{6,7},{8,9},{10,11},{12,13},{14,15},{16,17},{18,... | collective-permute-start | bytes 294920 | tf_op jit(solution)/shard_map/while/body/eval_jaxpr/ppermute | solution.py:38
  193.9 3.0 collective-permute-done.29
  196.9 2.8 collective-permute-start.24
  199.8 1.4 collective-permute-start.25
  202.2 4.6 %collective-permute-done.25 = f32[8,32,128]{2,1,0:T(8,128)S(1)} collective-permute-done((f32[8,32,128]{2,1,0:T(8,128)S(1)}, f32[8,32,128]{2,1,0:T(8,128)S(1)}, u32[]{:S(2)}, u32[]{:S(2)}) %collective-permute-start.25) | collective-permute-done | bytes 131104 | tf_op jit(solution)/shard_map/while/body/eval_jaxpr/ppermute | solution.py:41
  209.7 1.5 collective-permute-start.32
  212.5 1.9 collective-permute-start.30
  215.8 1.9 collective-permute-done.33
  218.3 3.1 collective-permute-done.31
  223.3 4.6 %collective-permute-start.36 = (f32[24,8,128]{2,1,0:T(8,128)S(1)}, f32[24,8,128]{2,1,0:T(8,128)S(1)}, u32[]{:S(2)}, u32[]{:S(2)}) collective-permute-start(f32[24,8,128]{2,1,0:T(8,128)S(1)} %get-tuple-element.123), channel_id=1, source_target_pairs={{0,1},{2,3},{4,5},{6,7},{8,9},{10,11},{12,13},{14,15},{16,17},{18,... | collective-permute-start | bytes 294920 | tf_op jit(solution)/shard_map/while/body/eval_jaxpr/ppermute | solution.py:38
  229.2 1.9 collective-permute-start.34
  231.1 1.5 collective-permute-start.35
  232.6 1.7 collective-permute-done.37
  234.9 3.0 collective-permute-done.35
  241.0 2.1 copy.66
  243.2 2.1 reshape.234
  245.2 22.8 %reduce-scatter.4.cloned.1.call-done = f32[32,1536]{1,0:T(8,128)} async-done(((f32[128,1536]{1,0:T(8,128)}), f32[32,1536]{1,0:T(8,128)}) %reduce-scatter.4.cloned.1.call-update) | async-done | bytes 196624
  270.7 1.9 stack.27
  272.7 3.3 stack.28
  275.9 5.6 %maximum_bitcast_fusion = f32[8,6,8,2,4,4,4]{6,0,5,2,4,1,3:T(8,128)} fusion(f32[1,6,4,8,4,8,4]{6,5,4,3,2,1,0:T(8,128)} %stack.28, f32[1,6,4,8,4,8,4]{6,5,4,3,2,1,0:T(8,128)S(1)} %stack.27), kind=kLoop, calls=%fused_computation | loop fusion | flops 49152 | bytes 393216 | tf_op jit(solution)/shard_map/transpose | solution.py:140
  281.5 17.0 %copy.60 = f32[8,6,8,2,4,4,4]{2,1,0,6,5,4,3:T(8,128)} copy(f32[8,6,8,2,4,4,4]{6,0,5,2,4,1,3:T(8,128)} %maximum_bitcast_fusion) | data formatting | bytes 393216 | tf_op jit(solution)/shard_map/transpose | solution.py:140
  298.5 3.0 reshape.229
  302.9 40.3 %all-reduce.12 = (f32[64,64]{0,1:T(8,128)S(1)}, f32[64,128]{1,0:T(8,128)}) all-reduce(f32[64,64]{0,1:T(8,128)S(1)} %convolution_bitcast_fusion, f32[64,128]{1,0:T(8,128)S(1)} %fusion.408), channel_id=1, replica_groups=mesh['shot'=4,'gx'=4,'gy'=2] {'shot','gx','gy'}, use_global_device_ids=true, to_apply=%region_1.2 | all-reduce | flops 12288 | bytes 98304 | tf_op jit(solution)/shard_map/psum | solution.py:260
  (177 shorter events, 59.5 us)
Async XLA Ops:
  7.2 17.8 %copy-start = (f32[64,128]{1,0:T(8,128)S(1)}, f32[64,128]{1,0:T(8,128)}, u32[]{:S(2)}) copy-start(f32[64,128]{1,0:T(8,128)} %param.13) | copy-start | bytes 98308
  7.2 260.8 %reduce-scatter.4.cloned.1.call-start = ((), (), s32[]{:S(2)}) async-start(), calls=%async_computation.1 | async-start | bytes 983040
  8.9 83.2 %collective-permute-start.12 = (f32[24,8,128]{2,1,0:T(8,128)}, f32[24,8,128]{2,1,0:T(8,128)}, u32[]{:S(2)}, u32[]{:S(2)}) collective-permute-start(f32[24,8,128]{2,1,0:T(8,128)} %get-tuple-element.145), channel_id=1, source_target_pairs={{0,1},{2,3},{4,5},{6,7},{8,9},{10,11},{12,13},{14,15},{16,17},{18,... | collective-permute-start | bytes 294920 | tf_op jit(solution)/shard_map/while/body/eval_jaxpr/ppermute | solution.py:38
  14.3 82.9 %collective-permute-start.13 = (f32[24,8,128]{2,1,0:T(8,128)}, f32[24,8,128]{2,1,0:T(8,128)}, u32[]{:S(2)}, u32[]{:S(2)}) collective-permute-start(f32[24,8,128]{2,1,0:T(8,128)} %get-tuple-element.146), channel_id=1, source_target_pairs={{1,0},{3,2},{5,4},{7,6},{9,8},{11,10},{13,12},{15,14},{17,16},{19,... | collective-permute-start | bytes 294920 | tf_op jit(solution)/shard_map/while/body/eval_jaxpr/ppermute | solution.py:41
  17.3 86.7 %collective-permute-start.6 = (f32[8,32,128]{2,1,0:T(8,128)}, f32[8,32,128]{2,1,0:T(8,128)}, u32[]{:S(2)}, u32[]{:S(2)}) collective-permute-start(f32[8,32,128]{2,1,0:T(8,128)} %get-tuple-element.143), channel_id=1, source_target_pairs={{0,2},{2,4},{4,6},{1,3},{3,5},{5,7},{8,10},{10,12},{12,14},{9,11},... | collective-permute-start | bytes 393224 | tf_op jit(solution)/shard_map/while/body/eval_jaxpr/ppermute | solution.py:38
  21.5 83.8 %collective-permute-start.7 = (f32[8,32,128]{2,1,0:T(8,128)}, f32[8,32,128]{2,1,0:T(8,128)}, u32[]{:S(2)}, u32[]{:S(2)}) collective-permute-start(f32[8,32,128]{2,1,0:T(8,128)} %get-tuple-element.144), channel_id=1, source_target_pairs={{2,0},{4,2},{6,4},{3,1},{5,3},{7,5},{10,8},{12,10},{14,12},{11,9},... | collective-permute-start | bytes 393224 | tf_op jit(solution)/shard_map/while/body/eval_jaxpr/ppermute | solution.py:41
  49.0 9.4 %copy-start.24 = (s32[3,1]{0,1:T(1,128)S(1)}, s32[3,1]{0,1:T(1,128)}, u32[]{:S(2)}) copy-start(s32[3,1]{0,1:T(1,128)} %param.18) | copy-start | bytes 40
  49.0 10.7 %copy-start.25 = (f32[3,1]{0,1:T(1,128)S(1)}, f32[3,1]{0,1:T(1,128)}, u32[]{:S(2)}) copy-start(f32[3,1]{0,1:T(1,128)} %param.19) | copy-start | bytes 40
  49.0 11.9 %copy-start.22 = (s32[1,3,2048]{2,0,1:T(1,128)S(1)}, s32[1,3,2048]{2,0,1:T(1,128)}, u32[]{:S(2)}) copy-start(s32[1,3,2048]{2,0,1:T(1,128)} %param.20) | copy-start | bytes 73732
  49.0 12.0 %copy-start.23 = (f32[1,3,2048]{2,0,1:T(1,128)S(1)}, f32[1,3,2048]{2,0,1:T(1,128)}, u32[]{:S(2)}) copy-start(f32[1,3,2048]{2,0,1:T(1,128)} %param.21) | copy-start | bytes 73732
  50.3 14.4 %copy-start.2 = (f32[2,24,32,32]{3,2,1,0:T(8,128)}, f32[2,24,32,32]{3,2,1,0:T(8,128)S(1)}, u32[]{:S(2)}) copy-start(f32[2,24,32,32]{3,2,1,0:T(8,128)S(1)} %pad_maximum_fusion) | copy-start | bytes 589828
  50.4 39.5 %collective-permute-start = (f32[2,24,32,32]{3,2,1,0:T(8,128)S(1)}, f32[2,24,32,32]{3,2,1,0:T(8,128)S(1)}, u32[]{:S(2)}, u32[]{:S(2)}) collective-permute-start(f32[2,24,32,32]{3,2,1,0:T(8,128)S(1)} %pad_maximum_fusion), channel_id=1, source_target_pairs={{0,24},{8,0},{16,8},{24,16},{1,25},{9,1},{17,9},{25,17},{2,26},{10... | collective-permute-start | bytes 589832 | tf_op jit(solution)/shard_map/ppermute | solution.py:25
  54.7 17.9 %copy-start.7 = (f32[24,32,128]{2,1,0:T(8,128)}, f32[24,32,128]{2,1,0:T(8,128)S(1)}, u32[]{:S(2)}) copy-start(f32[24,32,128]{2,1,0:T(8,128)S(1)} %get-tuple-element.118) | copy-start | bytes 1179652
  58.3 30.9 %copy-start.8 = (f32[24,32,128]{2,1,0:T(8,128)}, f32[24,32,128]{2,1,0:T(8,128)S(1)}, u32[]{:S(2)}) copy-start(f32[24,32,128]{2,1,0:T(8,128)S(1)} %get-tuple-element.114) | copy-start | bytes 1179652
  76.7 26.3 %copy-start.1 = (f32[1,24,32,128]{3,2,1,0:T(8,128)S(1)}, f32[1,24,32,128]{3,2,1,0:T(8,128)}, u32[]{:S(2)}) copy-start(f32[1,24,32,128]{3,2,1,0:T(8,128)} %param.14) | copy-start | bytes 1179652
  89.9 16.4 %copy-start.3 = (f32[2,24,32,32]{3,2,1,0:T(8,128)}, f32[2,24,32,32]{3,2,1,0:T(8,128)S(1)}, u32[]{:S(2)}) copy-start(f32[2,24,32,32]{3,2,1,0:T(8,128)S(1)} %collective-permute-done) | copy-start | bytes 589828
  90.2 19.7 %collective-permute-start.1 = (f32[2,24,32,64]{3,2,1,0:T(8,128)S(1)}, f32[2,24,32,64]{3,2,1,0:T(8,128)}, u32[]{:S(2)}, u32[]{:S(2)}) collective-permute-start(f32[2,24,32,64]{3,2,1,0:T(8,128)S(1)} %pad_maximum_fusion.1), channel_id=1, source_target_pairs={{0,16},{8,24},{16,0},{24,8},{1,17},{9,25},{17,1},{25,9},{2,18},{10... | collective-permute-start | bytes 1179656 | tf_op jit(solution)/shard_map/ppermute | solution.py:25
  92.0 44.0 %collective-permute-start.2 = (f32[4,32,128]{2,1,0:T(8,128)}, f32[4,32,128]{2,1,0:T(8,128)}, u32[]{:S(2)}, u32[]{:S(2)}) collective-permute-start(f32[4,32,128]{2,1,0:T(8,128)} %get-tuple-element.115), channel_id=1, source_target_pairs={{0,2},{2,4},{4,6},{1,3},{3,5},{5,7},{8,10},{10,12},{12,14},{9,11},... | collective-permute-start | bytes 196616 | tf_op jit(solution)/shard_map/while/body/eval_jaxpr/ppermute | solution.py:38
  97.2 25.4 %collective-permute-start.8 = (f32[24,4,128]{2,1,0:T(4,128)}, f32[24,4,128]{2,1,0:T(4,128)}, u32[]{:S(2)}, u32[]{:S(2)}) collective-permute-start(f32[24,4,128]{2,1,0:T(4,128)} %get-tuple-element.151), channel_id=1, source_target_pairs={{0,1},{2,3},{4,5},{6,7},{8,9},{10,11},{12,13},{14,15},{16,17},{18,... | collective-permute-start | bytes 147464 | tf_op jit(solution)/shard_map/while/body/eval_jaxpr/ppermute | solution.py:38
  104.0 20.0 %collective-permute-start.9 = (f32[24,4,128]{2,1,0:T(4,128)}, f32[24,4,128]{2,1,0:T(4,128)}, u32[]{:S(2)}, u32[]{:S(2)}) collective-permute-start(f32[24,4,128]{2,1,0:T(4,128)} %get-tuple-element.152), channel_id=1, source_target_pairs={{1,0},{3,2},{5,4},{7,6},{9,8},{11,10},{13,12},{15,14},{17,16},{19,... | collective-permute-start | bytes 147464 | tf_op jit(solution)/shard_map/while/body/eval_jaxpr/ppermute | solution.py:41
  115.9 20.2 %copy-start.19 = (f32[4,32,128]{2,1,0:T(8,128)S(1)}, f32[4,32,128]{2,1,0:T(8,128)}, u32[]{:S(2)}) copy-start(f32[4,32,128]{2,1,0:T(8,128)} %get-tuple-element.112) | copy-start | bytes 196612
  115.9 21.5 %copy-start.21 = (f32[24,4,128]{2,1,0:T(4,128)S(1)}, f32[24,4,128]{2,1,0:T(4,128)}, u32[]{:S(2)}) copy-start(f32[24,4,128]{2,1,0:T(4,128)} %get-tuple-element.131) | copy-start | bytes 147460
  115.9 26.2 %copy-start.16 = (f32[24,32,128]{2,1,0:T(8,128)S(1)}, f32[24,32,128]{2,1,0:T(8,128)}, u32[]{:S(2)}) copy-start(f32[24,32,128]{2,1,0:T(8,128)} %get-tuple-element.117) | copy-start | bytes 1179652
  115.9 13.2 %collective-permute-start.10 = (f32[24,4,128]{2,1,0:T(4,128)S(1)}, f32[24,4,128]{2,1,0:T(4,128)S(1)}, u32[]{:S(2)}, u32[]{:S(2)}) collective-permute-start(f32[24,4,128]{2,1,0:T(4,128)S(1)} %get-tuple-element.147), channel_id=1, source_target_pairs={{0,1},{2,3},{4,5},{6,7},{8,9},{10,11},{12,13},{14,15},{16,17},{18,... | collective-permute-start | bytes 147464 | tf_op jit(solution)/shard_map/ppermute | solution.py:38
  121.2 11.9 %collective-permute-start.11 = (f32[24,4,128]{2,1,0:T(4,128)S(1)}, f32[24,4,128]{2,1,0:T(4,128)S(1)}, u32[]{:S(2)}, u32[]{:S(2)}) collective-permute-start(f32[24,4,128]{2,1,0:T(4,128)S(1)} %get-tuple-element.148), channel_id=1, source_target_pairs={{1,0},{3,2},{5,4},{7,6},{9,8},{11,10},{13,12},{15,14},{17,16},{19,... | collective-permute-start | bytes 147464 | tf_op jit(solution)/shard_map/ppermute | solution.py:41
  122.7 14.7 %collective-permute-start.3 = (f32[4,32,128]{2,1,0:T(8,128)}, f32[4,32,128]{2,1,0:T(8,128)S(1)}, u32[]{:S(2)}, u32[]{:S(2)}) collective-permute-start(f32[4,32,128]{2,1,0:T(8,128)} %get-tuple-element.116), channel_id=1, source_target_pairs={{2,0},{4,2},{6,4},{3,1},{5,3},{7,5},{10,8},{12,10},{14,12},{11,9},... | collective-permute-start | bytes 196616 | tf_op jit(solution)/shard_map/while/body/eval_jaxpr/ppermute | solution.py:41
  124.0 82.9 %collective-permute-start.22 = (f32[4,32,128]{2,1,0:T(8,128)}, f32[4,32,128]{2,1,0:T(8,128)S(1)}, u32[]{:S(2)}, u32[]{:S(2)}) collective-permute-start(f32[4,32,128]{2,1,0:T(8,128)} %get-tuple-element.111), channel_id=1, source_target_pairs={{0,2},{2,4},{4,6},{1,3},{3,5},{5,7},{8,10},{10,12},{12,14},{9,11},... | collective-permute-start | bytes 196616 | tf_op jit(solution)/shard_map/while/body/eval_jaxpr/ppermute | solution.py:38
  129.2 12.9 %collective-permute-start.4 = (f32[4,32,128]{2,1,0:T(8,128)S(1)}, f32[4,32,128]{2,1,0:T(8,128)S(1)}, u32[]{:S(2)}, u32[]{:S(2)}) collective-permute-start(f32[4,32,128]{2,1,0:T(8,128)S(1)} %get-tuple-element.107), channel_id=1, source_target_pairs={{0,2},{2,4},{4,6},{1,3},{3,5},{5,7},{8,10},{10,12},{12,14},{9,11},... | collective-permute-start | bytes 196616 | tf_op jit(solution)/shard_map/ppermute | solution.py:38
  133.1 9.0 %collective-permute-start.5 = (f32[4,32,128]{2,1,0:T(8,128)S(1)}, f32[4,32,128]{2,1,0:T(8,128)S(1)}, u32[]{:S(2)}, u32[]{:S(2)}) collective-permute-start(f32[4,32,128]{2,1,0:T(8,128)S(1)} %get-tuple-element.108), channel_id=1, source_target_pairs={{2,0},{4,2},{6,4},{3,1},{5,3},{7,5},{10,8},{12,10},{14,12},{11,9},... | collective-permute-start | bytes 196616 | tf_op jit(solution)/shard_map/ppermute | solution.py:41
  136.0 70.8 %collective-permute-start.23 = (f32[4,32,128]{2,1,0:T(8,128)S(1)}, f32[4,32,128]{2,1,0:T(8,128)S(1)}, u32[]{:S(2)}, u32[]{:S(2)}) collective-permute-start(f32[4,32,128]{2,1,0:T(8,128)S(1)} %copy-done.19), channel_id=1, source_target_pairs={{2,0},{4,2},{6,4},{3,1},{5,3},{7,5},{10,8},{12,10},{14,12},{11,9},... | collective-permute-start | bytes 196616 | tf_op jit(solution)/shard_map/while/body/eval_jaxpr/ppermute | solution.py:41
  137.4 62.4 %collective-permute-start.26 = (f32[24,4,128]{2,1,0:T(4,128)S(1)}, f32[24,4,128]{2,1,0:T(4,128)S(1)}, u32[]{:S(2)}, u32[]{:S(2)}) collective-permute-start(f32[24,4,128]{2,1,0:T(4,128)S(1)} %copy-done.21), channel_id=1, source_target_pairs={{0,1},{2,3},{4,5},{6,7},{8,9},{10,11},{12,13},{14,15},{16,17},{18,... | collective-permute-start | bytes 147464 | tf_op jit(solution)/shard_map/while/body/eval_jaxpr/ppermute | solution.py:38
  145.7 3.9 %collective-permute-start.16 = (f32[24,8,128]{2,1,0:T(8,128)S(1)}, f32[24,8,128]{2,1,0:T(8,128)S(1)}, u32[]{:S(2)}, u32[]{:S(2)}) collective-permute-start(f32[24,8,128]{2,1,0:T(8,128)S(1)} %get-tuple-element.141), channel_id=1, source_target_pairs={{0,1},{2,3},{4,5},{6,7},{8,9},{10,11},{12,13},{14,15},{16,17},{18,... | collective-permute-start | bytes 294920 | tf_op jit(solution)/shard_map/while/body/eval_jaxpr/ppermute | solution.py:38
  147.4 7.0 %collective-permute-start.17 = (f32[24,8,128]{2,1,0:T(8,128)S(1)}, f32[24,8,128]{2,1,0:T(8,128)S(1)}, u32[]{:S(2)}, u32[]{:S(2)}) collective-permute-start(f32[24,8,128]{2,1,0:T(8,128)S(1)} %get-tuple-element.142), channel_id=1, source_target_pairs={{1,0},{3,2},{5,4},{7,6},{9,8},{11,10},{13,12},{15,14},{17,16},{19,... | collective-permute-start | bytes 294920 | tf_op jit(solution)/shard_map/while/body/eval_jaxpr/ppermute | solution.py:41
  149.6 7.3 %collective-permute-start.14 = (f32[8,32,128]{2,1,0:T(8,128)S(1)}, f32[8,32,128]{2,1,0:T(8,128)S(1)}, u32[]{:S(2)}, u32[]{:S(2)}) collective-permute-start(f32[8,32,128]{2,1,0:T(8,128)S(1)} %get-tuple-element.139), channel_id=1, source_target_pairs={{0,2},{2,4},{4,6},{1,3},{3,5},{5,7},{8,10},{10,12},{12,14},{9,11},... | collective-permute-start | bytes 393224 | tf_op jit(solution)/shard_map/while/body/eval_jaxpr/ppermute | solution.py:38
  154.4 7.2 %collective-permute-start.15 = (f32[8,32,128]{2,1,0:T(8,128)S(1)}, f32[8,32,128]{2,1,0:T(8,128)S(1)}, u32[]{:S(2)}, u32[]{:S(2)}) collective-permute-start(f32[8,32,128]{2,1,0:T(8,128)S(1)} %get-tuple-element.140), channel_id=1, source_target_pairs={{2,0},{4,2},{6,4},{3,1},{5,3},{7,5},{10,8},{12,10},{14,12},{11,9},... | collective-permute-start | bytes 393224 | tf_op jit(solution)/shard_map/while/body/eval_jaxpr/ppermute | solution.py:41
  164.3 6.1 %collective-permute-start.20 = (f32[24,8,128]{2,1,0:T(8,128)S(1)}, f32[24,8,128]{2,1,0:T(8,128)S(1)}, u32[]{:S(2)}, u32[]{:S(2)}) collective-permute-start(f32[24,8,128]{2,1,0:T(8,128)S(1)} %get-tuple-element.137), channel_id=1, source_target_pairs={{0,1},{2,3},{4,5},{6,7},{8,9},{10,11},{12,13},{14,15},{16,17},{18,... | collective-permute-start | bytes 294920 | tf_op jit(solution)/shard_map/while/body/eval_jaxpr/ppermute | solution.py:38
  168.2 6.5 %collective-permute-start.21 = (f32[24,8,128]{2,1,0:T(8,128)S(1)}, f32[24,8,128]{2,1,0:T(8,128)S(1)}, u32[]{:S(2)}, u32[]{:S(2)}) collective-permute-start(f32[24,8,128]{2,1,0:T(8,128)S(1)} %get-tuple-element.138), channel_id=1, source_target_pairs={{1,0},{3,2},{5,4},{7,6},{9,8},{11,10},{13,12},{15,14},{17,16},{19,... | collective-permute-start | bytes 294920 | tf_op jit(solution)/shard_map/while/body/eval_jaxpr/ppermute | solution.py:41
  170.4 6.4 %collective-permute-start.18 = (f32[8,32,128]{2,1,0:T(8,128)S(1)}, f32[8,32,128]{2,1,0:T(8,128)S(1)}, u32[]{:S(2)}, u32[]{:S(2)}) collective-permute-start(f32[8,32,128]{2,1,0:T(8,128)S(1)} %get-tuple-element.135), channel_id=1, source_target_pairs={{0,2},{2,4},{4,6},{1,3},{3,5},{5,7},{8,10},{10,12},{12,14},{9,11},... | collective-permute-start | bytes 393224 | tf_op jit(solution)/shard_map/while/body/eval_jaxpr/ppermute | solution.py:38
  174.7 6.8 %collective-permute-start.19 = (f32[8,32,128]{2,1,0:T(8,128)S(1)}, f32[8,32,128]{2,1,0:T(8,128)S(1)}, u32[]{:S(2)}, u32[]{:S(2)}) collective-permute-start(f32[8,32,128]{2,1,0:T(8,128)S(1)} %get-tuple-element.136), channel_id=1, source_target_pairs={{2,0},{4,2},{6,4},{3,1},{5,3},{7,5},{10,8},{12,10},{14,12},{11,9},... | collective-permute-start | bytes 393224 | tf_op jit(solution)/shard_map/while/body/eval_jaxpr/ppermute | solution.py:41
  181.6 1.0 copy-start.4
  181.6 1.1 copy-start.13
  181.6 1.2 copy-start.14
  181.7 1.3 copy-start.17
  183.0 9.6 %copy-start.20 = (f32[24,4,128]{2,1,0:T(4,128)S(1)}, f32[24,4,128]{2,1,0:T(4,128)}, u32[]{:S(2)}) copy-start(f32[24,4,128]{2,1,0:T(4,128)} %get-tuple-element.132) | copy-start | bytes 147460
  184.6 16.7 %copy-start.9 = (f32[24,32,128]{2,1,0:T(8,128)S(1)}, f32[24,32,128]{2,1,0:T(8,128)}, u32[]{:S(2)}) copy-start(f32[24,32,128]{2,1,0:T(8,128)} %copy-done.8) | copy-start | bytes 1179652
  186.4 6.1 %collective-permute-start.28 = (f32[24,8,128]{2,1,0:T(8,128)S(1)}, f32[24,8,128]{2,1,0:T(8,128)S(1)}, u32[]{:S(2)}, u32[]{:S(2)}) collective-permute-start(f32[24,8,128]{2,1,0:T(8,128)S(1)} %get-tuple-element.133), channel_id=1, source_target_pairs={{0,1},{2,3},{4,5},{6,7},{8,9},{10,11},{12,13},{14,15},{16,17},{18,... | collective-permute-start | bytes 294920 | tf_op jit(solution)/shard_map/while/body/eval_jaxpr/ppermute | solution.py:38
  190.4 6.5 %collective-permute-start.29 = (f32[24,8,128]{2,1,0:T(8,128)S(1)}, f32[24,8,128]{2,1,0:T(8,128)S(1)}, u32[]{:S(2)}, u32[]{:S(2)}) collective-permute-start(f32[24,8,128]{2,1,0:T(8,128)S(1)} %get-tuple-element.134), channel_id=1, source_target_pairs={{1,0},{3,2},{5,4},{7,6},{9,8},{11,10},{13,12},{15,14},{17,16},{19,... | collective-permute-start | bytes 294920 | tf_op jit(solution)/shard_map/while/body/eval_jaxpr/ppermute | solution.py:41
  192.6 8.7 %collective-permute-start.27 = (f32[24,4,128]{2,1,0:T(4,128)S(1)}, f32[24,4,128]{2,1,0:T(4,128)S(1)}, u32[]{:S(2)}, u32[]{:S(2)}) collective-permute-start(f32[24,4,128]{2,1,0:T(4,128)S(1)} %copy-done.20), channel_id=1, source_target_pairs={{1,0},{3,2},{5,4},{7,6},{9,8},{11,10},{13,12},{15,14},{17,16},{19,... | collective-permute-start | bytes 147464 | tf_op jit(solution)/shard_map/while/body/eval_jaxpr/ppermute | solution.py:41
  196.9 5.3 %collective-permute-start.24 = (f32[8,32,128]{2,1,0:T(8,128)S(1)}, f32[8,32,128]{2,1,0:T(8,128)S(1)}, u32[]{:S(2)}, u32[]{:S(2)}) collective-permute-start(f32[8,32,128]{2,1,0:T(8,128)S(1)} %get-tuple-element.129), channel_id=1, source_target_pairs={{0,2},{2,4},{4,6},{1,3},{3,5},{5,7},{8,10},{10,12},{12,14},{9,11},... | collective-permute-start | bytes 393224 | tf_op jit(solution)/shard_map/while/body/eval_jaxpr/ppermute | solution.py:38
  199.8 7.1 %copy-start.15 = (f32[24,32,128]{2,1,0:T(8,128)S(1)}, f32[24,32,128]{2,1,0:T(8,128)}, u32[]{:S(2)}) copy-start(f32[24,32,128]{2,1,0:T(8,128)} %get-tuple-element.113) | copy-start | bytes 1179652
  199.8 7.0 %collective-permute-start.25 = (f32[8,32,128]{2,1,0:T(8,128)S(1)}, f32[8,32,128]{2,1,0:T(8,128)S(1)}, u32[]{:S(2)}, u32[]{:S(2)}) collective-permute-start(f32[8,32,128]{2,1,0:T(8,128)S(1)} %get-tuple-element.130), channel_id=1, source_target_pairs={{2,0},{4,2},{6,4},{3,1},{5,3},{7,5},{10,8},{12,10},{14,12},{11,9},... | collective-permute-start | bytes 393224 | tf_op jit(solution)/shard_map/while/body/eval_jaxpr/ppermute | solution.py:41
  206.8 1.0 copy-start.11
  206.9 1.1 copy-start.12
  209.7 6.1 %collective-permute-start.32 = (f32[24,8,128]{2,1,0:T(8,128)S(1)}, f32[24,8,128]{2,1,0:T(8,128)S(1)}, u32[]{:S(2)}, u32[]{:S(2)}) collective-permute-start(f32[24,8,128]{2,1,0:T(8,128)S(1)} %get-tuple-element.127), channel_id=1, source_target_pairs={{0,1},{2,3},{4,5},{6,7},{8,9},{10,11},{12,13},{14,15},{16,17},{18,... | collective-permute-start | bytes 294920 | tf_op jit(solution)/shard_map/while/body/eval_jaxpr/ppermute | solution.py:38
  211.2 6.5 %collective-permute-start.33 = (f32[24,8,128]{2,1,0:T(8,128)S(1)}, f32[24,8,128]{2,1,0:T(8,128)S(1)}, u32[]{:S(2)}, u32[]{:S(2)}) collective-permute-start(f32[24,8,128]{2,1,0:T(8,128)S(1)} %get-tuple-element.128), channel_id=1, source_target_pairs={{1,0},{3,2},{5,4},{7,6},{9,8},{11,10},{13,12},{15,14},{17,16},{19,... | collective-permute-start | bytes 294920 | tf_op jit(solution)/shard_map/while/body/eval_jaxpr/ppermute | solution.py:41
  212.5 5.7 %collective-permute-start.30 = (f32[8,32,128]{2,1,0:T(8,128)S(1)}, f32[8,32,128]{2,1,0:T(8,128)S(1)}, u32[]{:S(2)}, u32[]{:S(2)}) collective-permute-start(f32[8,32,128]{2,1,0:T(8,128)S(1)} %get-tuple-element.125), channel_id=1, source_target_pairs={{0,2},{2,4},{4,6},{1,3},{3,5},{5,7},{8,10},{10,12},{12,14},{9,11},... | collective-permute-start | bytes 393224 | tf_op jit(solution)/shard_map/while/body/eval_jaxpr/ppermute | solution.py:38
  214.5 6.9 %collective-permute-start.31 = (f32[8,32,128]{2,1,0:T(8,128)S(1)}, f32[8,32,128]{2,1,0:T(8,128)S(1)}, u32[]{:S(2)}, u32[]{:S(2)}) collective-permute-start(f32[8,32,128]{2,1,0:T(8,128)S(1)} %get-tuple-element.126), channel_id=1, source_target_pairs={{2,0},{4,2},{6,4},{3,1},{5,3},{7,5},{10,8},{12,10},{14,12},{11,9},... | collective-permute-start | bytes 393224 | tf_op jit(solution)/shard_map/while/body/eval_jaxpr/ppermute | solution.py:41
  223.3 9.3 %collective-permute-start.36 = (f32[24,8,128]{2,1,0:T(8,128)S(1)}, f32[24,8,128]{2,1,0:T(8,128)S(1)}, u32[]{:S(2)}, u32[]{:S(2)}) collective-permute-start(f32[24,8,128]{2,1,0:T(8,128)S(1)} %get-tuple-element.123), channel_id=1, source_target_pairs={{0,1},{2,3},{4,5},{6,7},{8,9},{10,11},{12,13},{14,15},{16,17},{18,... | collective-permute-start | bytes 294920 | tf_op jit(solution)/shard_map/while/body/eval_jaxpr/ppermute | solution.py:38
  227.8 6.5 %collective-permute-start.37 = (f32[24,8,128]{2,1,0:T(8,128)S(1)}, f32[24,8,128]{2,1,0:T(8,128)S(1)}, u32[]{:S(2)}, u32[]{:S(2)}) collective-permute-start(f32[24,8,128]{2,1,0:T(8,128)S(1)} %get-tuple-element.124), channel_id=1, source_target_pairs={{1,0},{3,2},{5,4},{7,6},{9,8},{11,10},{13,12},{15,14},{17,16},{19,... | collective-permute-start | bytes 294920 | tf_op jit(solution)/shard_map/while/body/eval_jaxpr/ppermute | solution.py:41
  229.2 5.7 %collective-permute-start.34 = (f32[8,32,128]{2,1,0:T(8,128)S(1)}, f32[8,32,128]{2,1,0:T(8,128)S(1)}, u32[]{:S(2)}, u32[]{:S(2)}) collective-permute-start(f32[8,32,128]{2,1,0:T(8,128)S(1)} %get-tuple-element.121), channel_id=1, source_target_pairs={{0,2},{2,4},{4,6},{1,3},{3,5},{5,7},{8,10},{10,12},{12,14},{9,11},... | collective-permute-start | bytes 393224 | tf_op jit(solution)/shard_map/while/body/eval_jaxpr/ppermute | solution.py:38
  231.1 6.9 %collective-permute-start.35 = (f32[8,32,128]{2,1,0:T(8,128)S(1)}, f32[8,32,128]{2,1,0:T(8,128)S(1)}, u32[]{:S(2)}, u32[]{:S(2)}) collective-permute-start(f32[8,32,128]{2,1,0:T(8,128)S(1)} %get-tuple-element.122), channel_id=1, source_target_pairs={{2,0},{4,2},{6,4},{3,1},{5,3},{7,5},{10,8},{12,10},{14,12},{11,9},... | collective-permute-start | bytes 393224 | tf_op jit(solution)/shard_map/while/body/eval_jaxpr/ppermute | solution.py:41
  245.2 24.4 %copy-start.5 = (f32[1,24,32,32]{3,2,1,0:T(8,128)S(1)}, f32[1,24,32,32]{3,2,1,0:T(8,128)}, u32[]{:S(2)}) copy-start(f32[1,24,32,32]{3,2,1,0:T(8,128)} %div.74) | copy-start | bytes 294916
  245.2 24.4 %copy-start.6 = (f32[1,24,32,32]{3,2,1,0:T(8,128)S(1)}, f32[1,24,32,32]{3,2,1,0:T(8,128)}, u32[]{:S(2)}) copy-start(f32[1,24,32,32]{3,2,1,0:T(8,128)} %div.72) | copy-start | bytes 294916
  298.5 3.9 %copy-start.18 = (f32[64,64]{1,0:T(8,128)S(1)}, f32[64,64]{1,0:T(8,128)}, u32[]{:S(2)}) copy-start(f32[64,64]{1,0:T(8,128)} %param.12) | copy-start | bytes 49156
  (1 other events, 1.0 us)
Sparse Core Ops, SparseCore 0:
  245.4 22.6 reduce-scatter.3
